TPU v7x, 128 devices: a whole 4x4x4 slice. The times are simulated.
128 devices in a mesh: row: 4 (over z), col: 32 (over x, y, core).
Axes of the slice: x: 4, y: 4, z: 4, core: 2. Of those that a mesh axis runs over, the one named last changes fastest.
Arguments:
- fields: bfloat16 [8, 256, 32, 32, 128], P('row', 'col'), may hold values from -6 to 6
- wet_mask: int32 [8, 256], P('row', 'col'), may hold values from 0 to 1, as said below
- seam_flags: int32 [8, 256, 2], P('row', 'col'), may hold values from 0 to 1, as said below
- wet_list: int32 [1024], P(('row', 'col')), may hold values from 0 to 2047, as said below
- kernel_one: bfloat16 [3, 3, 128, 128], replicated, may hold values from -0.1875 to 0.1875
- bias_one: float32 [128], replicated, may hold values from -3 to 3
- kernel_two: bfloat16 [3, 3, 128, 128], replicated, may hold values from -0.1875 to 0.1875
- bias_two: float32 [128], replicated, may hold values from -3 to 3
- mixing: bfloat16 [128, 128], replicated, may hold values from -0.5 to 0.5
Outputs:
- updated: bfloat16 [1024, 32, 32, 128], P(('row', 'col'))
Inputs may be any that keep to these rules, and one draw needn't show every extreme that they name: `wet_mask`: every group of 2 tile rows holds exactly 256 wet tiles, and in every such group some block of 2 x 8 tiles starting at a tile column k * 8 is all wet. `wet_list`: number the wet tiles of tile-row group r (tile rows r * 2 to r * 2 + 1) from 0: block by block along the tile columns (blocks of 2 x 8 tiles starting at tile columns k * 8), within a block row by row. Slot (r * 32 + c) * 8 + s holds the tile number (tile row times 256 plus tile column) of that group's wet tile c + 32 * s. `seam_flags`: nonzero only on the west side of tiles whose tile column is a positive multiple of 8 and on the east side of the tile to their west, both with the same value.
All inputs are finite; a program needn't handle non-finite values.
Results may differ from a plain program's by a relative error of at most 0.0039.
Values may be sent and summed in bfloat16 or wider, within the bound.
No kernel may reach another device: no remote copies, remote signals or barrier semaphores. Data moves between devices by JAX's collectives and lax.ppermute only.
A program may use at most 128 MiB of HBM per device.

v0:
```python
import functools

import jax
import jax.numpy as jnp
from jax import lax
from jax.experimental import pallas as pl
from jax.experimental.pallas import tpu as pltpu
from jax.sharding import PartitionSpec as P

F32 = jnp.float32
BF16 = jnp.bfloat16
VMEM_LIMIT = 56 * 1024 * 1024
WHOLE = pl.BlockSpec(memory_space=pltpu.VMEM)
SCALARS = pl.BlockSpec(memory_space=pltpu.SMEM)
IN_PLACE = pl.BlockSpec(memory_space=pl.ANY)


def dot(a, b):
    return jnp.dot(a, b, preferred_element_type=F32)


def gelu(x):
    u = x * (0.7978845608028654 + 0.03567740813636141 * (x * x))
    half = 0.5 * x
    return half + half * jnp.tanh(u)


def fill_weights(k_ref, w_ref):
    ch = k_ref.shape[2]
    zero = jnp.zeros((ch, 3 * ch), BF16)
    w_ref[3 * ch :, : 3 * ch] = zero
    w_ref[:ch, 3 * ch :] = zero
    for dy in range(3):
        for dx in range(3):
            block = k_ref[dy, dx]
            w_ref[dy * ch : (dy + 1) * ch, dx * ch : (dx + 1) * ch] = block
            w_ref[(dy + 1) * ch : (dy + 2) * ch, (3 + dx) * ch : (4 + dx) * ch] = block


def fill_edges(ext_ref, flag_ref, side, k_ref, dx, pad_ref, z_ref, tr_dev, tile):
    ext = ext_ref[...].astype(F32)
    rows = lax.broadcasted_iota(jnp.int32, (tile, tile), 0)
    cols = lax.broadcasted_iota(jnp.int32, (tile, tile), 1)
    flip = jnp.where(rows + cols == tile - 1, 1.0, 0.0).astype(BF16)
    for i in range(tr_dev):
        part = ext[i * tile : i * tile + tile + 2]
        pad_ref[0 : tile + 2] = part
        middle = pad_ref[1 : tile + 1]
        turned = dot(flip, middle.astype(BF16))
        pad_ref[1 : tile + 1] = jnp.where(flag_ref[2 * i + side] == 1, turned, middle)
        total = dot(pad_ref[0:tile].astype(BF16), k_ref[0, dx])
        total += dot(pad_ref[1 : tile + 1].astype(BF16), k_ref[1, dx])
        total += dot(pad_ref[2 : tile + 2].astype(BF16), k_ref[2, dx])
        z_ref[i * tile : (i + 1) * tile] = total


def conv_pair(window, w_ref, bias, zw_ref, ze_ref, row):
    ch = window[0].shape[1]
    width = window[0].shape[0]
    z = dot(jnp.concatenate(window, axis=1), w_ref[...])
    lane_row = lax.broadcasted_iota(jnp.int32, (8, ch), 0)
    outs = []
    for ro in range(2):
        base = 3 * ro * ch
        left = pltpu.roll(z[:, base : base + ch], 1, 0)
        right = pltpu.roll(z[:, base + 2 * ch : base + 3 * ch], width - 1, 0)
        west = zw_ref[pl.ds(row + ro, 1), :]
        east = ze_ref[pl.ds(row + ro, 1), :]
        left = jnp.concatenate([jnp.where(lane_row == 0, west, left[:8]), left[8:]], axis=0)
        right = jnp.concatenate(
            [right[: width - 8], jnp.where(lane_row == 7, east, right[width - 8 :])], axis=0
        )
        outs.append(z[:, base + ch : base + 2 * ch] + left + right + bias)
    return outs


def span_of(height):
    return height // 4


def first_kernel(
    wet_ref, flag_ref, fields_ref, north_ref, south_ref, west_ref, east_ref, k_ref, b_ref,
    hid_out, lcol_ref, rcol_ref,
    f_ref, x_ref, hid_ref, w_ref, pad_ref, zw_ref, ze_ref, m_ref, lc_ref, rc_ref, in_sems, out_sems,
):
    tr_dev, tc_dev, tile, _, ch = fields_ref.shape
    width = tc_dev * tile
    height = tr_dev * tile
    span = span_of(height)
    loads = [
        pltpu.make_async_copy(fields_ref.at[i], f_ref.at[i], in_sems.at[i]) for i in range(tr_dev)
    ]
    for load in loads:
        load.start()
    fill_weights(k_ref, w_ref)
    fill_edges(west_ref, flag_ref, 0, k_ref, 0, pad_ref, zw_ref, tr_dev, tile)
    fill_edges(east_ref, flag_ref, 1, k_ref, 2, pad_ref, ze_ref, tr_dev, tile)
    x_ref[0] = north_ref[...]
    x_ref[height + 1] = south_ref[...]
    bias = b_ref[...]

    def fill(i):
        loads[i].wait()
        for j in range(tc_dev):
            wet = wet_ref[i * tc_dev + j].astype(F32)
            scale = jnp.full((1, ch), 1.0, F32) * wet
            m_ref[i, j * tile : (j + 1) * tile] = jnp.broadcast_to(scale, (tile, ch))
            x_ref[1 + i * tile : 1 + (i + 1) * tile, j * tile : (j + 1) * tile] = (
                f_ref[i, j] * scale.astype(BF16)[None]
            )

    def step(p, carry):
        row = 2 * p
        window = [x_ref[row + k] for k in range(4)]
        outs = conv_pair(window, w_ref, bias, zw_ref, ze_ref, row)
        for ro in range(2):
            value = gelu(outs[ro]) * m_ref[p // (tile // 2)]
            hid_ref[row + ro] = value.astype(BF16)
            lc_ref[pl.ds(row + ro, 1), :] = value[0:1]
            rc_ref[pl.ds(row + ro, 1), :] = value[width - 1 : width]
        return carry

    stores = [
        pltpu.make_async_copy(
            hid_ref.at[pl.ds(g * span, span)], hid_out.at[pl.ds(g * span, span)], out_sems.at[g]
        )
        for g in range(4)
    ]
    filled = 0
    for g in range(4):
        while filled < tr_dev and (g + 1) * span >= filled * tile:
            fill(filled)
            filled += 1
        lax.fori_loop(g * span // 2, (g + 1) * span // 2, step, 0, unroll=4)
        stores[g].start()
    lcol_ref[...] = lc_ref[...].astype(BF16)
    rcol_ref[...] = rc_ref[...].astype(BF16)
    for store in stores:
        store.wait()


def second_kernel(
    dst_ref, flag_ref, hid_hbm, fields_ref, north_ref, south_ref, west_ref, east_ref, k_ref, b_ref,
    mix_ref, keep_ref, give_ref,
    hid_ref, out_ref, w_ref, pad_ref, zw_ref, ze_ref, mm_ref, hid_sems, in_sems, sems,
):
    tr_dev, tc_dev, tile, _, ch = fields_ref.shape
    width = tc_dev * tile
    height = tr_dev * tile
    span = span_of(height)
    slots = keep_ref.shape[0]
    hid_loads = [
        pltpu.make_async_copy(
            hid_hbm.at[pl.ds(g * span, span)], hid_ref.at[pl.ds(1 + g * span, span)], hid_sems.at[g]
        )
        for g in range(4)
    ]
    loads = [
        pltpu.make_async_copy(fields_ref.at[i], out_ref.at[i], in_sems.at[i]) for i in range(tr_dev)
    ]
    hid_loads[0].start()
    hid_loads[1].start()
    loads[0].start()
    hid_loads[2].start()
    hid_loads[3].start()
    for load in loads[1:]:
        load.start()
    fill_weights(k_ref, w_ref)
    fill_edges(west_ref, flag_ref, 0, k_ref, 0, pad_ref, zw_ref, tr_dev, tile)
    fill_edges(east_ref, flag_ref, 1, k_ref, 2, pad_ref, ze_ref, tr_dev, tile)
    zero = jnp.zeros((ch, ch), BF16)
    mm_ref[:ch, :ch] = mix_ref[...]
    mm_ref[ch:, ch:] = mix_ref[...]
    mm_ref[:ch, ch:] = zero
    mm_ref[ch:, :ch] = zero
    hid_ref[0] = north_ref[...]
    hid_ref[height + 1] = south_ref[...]
    bias = b_ref[...]

    def copies(i, act):
        for j in range(tc_dev):
            k = i * tc_dev + j
            target = dst_ref[k]

            @pl.when((target >= 0) & (target < slots))
            def _():
                act(pltpu.make_async_copy(out_ref.at[i, j], keep_ref.at[target], sems.at[k]))

            @pl.when(target >= slots)
            def _():
                act(pltpu.make_async_copy(out_ref.at[i, j], give_ref.at[target - slots], sems.at[k]))

    def step(p, carry):
        row = 2 * p
        i = row // tile
        inner = row % tile
        window = [hid_ref[row + k] for k in range(4)]
        outs = conv_pair(window, w_ref, bias, zw_ref, ze_ref, row)
        branch = jnp.concatenate([gelu(o).astype(BF16) for o in outs], axis=1)
        mixed = dot(branch, mm_ref[...])
        for ro in range(2):
            own = out_ref[i, :, inner + ro].reshape(width, ch).astype(F32)
            total = (own + mixed[:, ro * ch : (ro + 1) * ch]).astype(BF16)
            out_ref[i, :, inner + ro] = total.reshape(tc_dev, tile, ch)
        return carry

    hid_loads[0].wait()
    for g in range(4):
        if g < 3:
            hid_loads[g + 1].wait()
        if g * span % tile == 0:
            loads[g * span // tile].wait()
        lax.fori_loop(g * span // 2, (g + 1) * span // 2, step, 0, unroll=4)
        if (g + 1) * span % tile == 0:
            copies(g * span // tile, lambda c: c.start())
    for i in range(tr_dev):
        copies(i, lambda c: c.wait())


def scatter_kernel(dst_ref, src_ref, held_ref, out_ref, buf_ref, in_sems, sems):
    def each(act):
        for k in range(src_ref.shape[0]):

            @pl.when(dst_ref[k] >= 0)
            def _():
                act(k)

    def load(k):
        return pltpu.make_async_copy(src_ref.at[k], buf_ref.at[k], in_sems.at[k])

    def store(k):
        return pltpu.make_async_copy(buf_ref.at[k], out_ref.at[dst_ref[k]], sems.at[k])

    def turn(k):
        load(k).wait()
        store(k).start()

    each(lambda k: load(k).start())
    each(turn)
    each(lambda k: store(k).wait())


def gather_kernel(idx_ref, src_ref, out_ref, buf_ref, in_sems, sems):
    count = out_ref.shape[0]

    def load(k):
        return pltpu.make_async_copy(src_ref.at[idx_ref[k]], buf_ref.at[k], in_sems.at[k])

    def store(k):
        return pltpu.make_async_copy(buf_ref.at[k], out_ref.at[k], sems.at[k])

    for k in range(count):
        load(k).start()
    for k in range(count):
        load(k).wait()
        store(k).start()
    for k in range(count):
        store(k).wait()


def shifted(x, axis, step):
    count = lax.axis_size(axis)
    pairs = [(i, i + step) for i in range(count) if 0 <= i + step < count]
    return lax.ppermute(x, axis, pairs)


def halos(top, bottom, left, right):
    north = shifted(bottom, "row", 1)
    south = shifted(top, "row", -1)
    left = jnp.concatenate([north[:1], left, south[:1]], axis=0)
    right = jnp.concatenate([north[-1:], right, south[-1:]], axis=0)
    return north, south, shifted(right, "col", 1), shifted(left, "col", -1)


def on_device(
    fields, wet_mask, seam_flags, wet_list, kernel_one, bias_one, kernel_two, bias_two, mixing
):
    tr_dev, tc_dev, tile, _, ch = fields.shape
    face = tr_dev * tc_dev
    wet_dev = wet_list.shape[0]
    columns = lax.axis_size("col")
    chips = columns // 2
    width, height = tc_dev * tile, tr_dev * tile
    me = lax.axis_index("col")
    core = me % 2
    wet = wet_mask.reshape(face)
    flags = jnp.stack([seam_flags[:, 0, 0], seam_flags[:, tc_dev - 1, 1]], axis=1).reshape(-1)

    total = jnp.broadcast_to(jnp.sum(wet), (columns, 1, 1))
    counts = lax.all_to_all(total, "col", split_axis=0, concat_axis=0, tiled=True).reshape(columns)
    cids = jnp.arange(columns)
    start = jnp.sum(jnp.where(cids < me, counts, 0))
    mate = me ^ 1
    mate_start = jnp.sum(jnp.where(cids < mate, counts, 0))
    mate_count = jnp.sum(jnp.where(cids == mate, counts, 0))
    ids = jnp.arange(face)
    local = jnp.sum(jnp.where(ids[None, :] < ids[:, None], wet[None, :], 0), axis=1)
    rank = start + local
    slot = (rank % columns) // 2
    dst = jnp.where(wet == 1, jnp.where(rank % 2 == core, slot, chips + local // 2), -1)
    half = face // 2
    mate_local = 2 * jnp.arange(half) + (mate_start + core) % 2
    mate_dst = jnp.where(mate_local < mate_count, ((mate_start + mate_local) % columns) // 2, -1)
    source_chip = (wet_list % (tc_dev * columns)) // (2 * tc_dev)

    scale = wet_mask.astype(BF16)
    top = (fields[0, :, 0] * scale[0, :, None, None]).reshape(width, ch)
    bottom = (fields[-1, :, -1] * scale[-1, :, None, None]).reshape(width, ch)
    left = (fields[:, 0, :, 0] * scale[:, 0, None, None]).reshape(height, ch)
    right = (fields[:, -1, :, -1] * scale[:, -1, None, None]).reshape(height, ch)
    params = pltpu.CompilerParams(vmem_limit_bytes=VMEM_LIMIT)
    hid, lcol, rcol = pl.pallas_call(
        first_kernel,
        out_shape=(
            jax.ShapeDtypeStruct((height, width, ch), BF16),
            jax.ShapeDtypeStruct((height, ch), BF16),
            jax.ShapeDtypeStruct((height, ch), BF16),
        ),
        in_specs=[SCALARS, SCALARS, IN_PLACE] + [WHOLE] * 6,
        out_specs=(IN_PLACE, WHOLE, WHOLE),
        scratch_shapes=[
            pltpu.VMEM(fields.shape, BF16),
            pltpu.VMEM((height + 2, width, ch), BF16),
            pltpu.VMEM((height, width, ch), BF16),
            pltpu.VMEM((4 * ch, 6 * ch), BF16),
            pltpu.VMEM((tile + 8, ch), F32),
            pltpu.VMEM((height, ch), F32),
            pltpu.VMEM((height, ch), F32),
            pltpu.VMEM((tr_dev, width, ch), F32),
            pltpu.VMEM((height, ch), F32),
            pltpu.VMEM((height, ch), F32),
            pltpu.SemaphoreType.DMA((tr_dev,)),
            pltpu.SemaphoreType.DMA((4,)),
        ],
        compiler_params=params,
        name="first_conv",
    )(wet, flags, fields, *halos(top, bottom, left, right), kernel_one, bias_one[None])

    tile_shape = (tile, tile, ch)
    keep, give = pl.pallas_call(
        second_kernel,
        out_shape=(
            jax.ShapeDtypeStruct((chips,) + tile_shape, BF16),
            jax.ShapeDtypeStruct((half,) + tile_shape, BF16),
        ),
        in_specs=[SCALARS, SCALARS, IN_PLACE, IN_PLACE] + [WHOLE] * 7,
        out_specs=(IN_PLACE, IN_PLACE),
        scratch_shapes=[
            pltpu.VMEM((height + 2, width, ch), BF16),
            pltpu.VMEM((tr_dev, tc_dev) + tile_shape, BF16),
            pltpu.VMEM((4 * ch, 6 * ch), BF16),
            pltpu.VMEM((tile + 8, ch), F32),
            pltpu.VMEM((height, ch), F32),
            pltpu.VMEM((height, ch), F32),
            pltpu.VMEM((2 * ch, 2 * ch), BF16),
            pltpu.SemaphoreType.DMA((4,)),
            pltpu.SemaphoreType.DMA((tr_dev,)),
            pltpu.SemaphoreType.DMA((face,)),
        ],
        compiler_params=params,
        name="second_conv",
    )(
        dst, flags, hid, fields, *halos(hid[0], hid[-1], lcol, rcol),
        kernel_two, bias_two[None], mixing,
    )

    taken = lax.ppermute(give, "col", [(i, i ^ 1) for i in range(columns)])
    sending = pl.pallas_call(
        scatter_kernel,
        out_shape=jax.ShapeDtypeStruct(keep.shape, BF16),
        in_specs=[SCALARS, IN_PLACE, IN_PLACE],
        out_specs=IN_PLACE,
        scratch_shapes=[
            pltpu.VMEM((half,) + tile_shape, BF16),
            pltpu.SemaphoreType.DMA((half,)),
            pltpu.SemaphoreType.DMA((half,)),
        ],
        input_output_aliases={2: 0},
        name="merge_mate",
    )(mate_dst, taken, keep)
    groups = [[2 * k + c for k in range(chips)] for c in range(2)]
    arrived = lax.all_to_all(
        sending, "col", split_axis=0, concat_axis=0, tiled=True, axis_index_groups=groups
    )
    return pl.pallas_call(
        gather_kernel,
        out_shape=jax.ShapeDtypeStruct((wet_dev,) + tile_shape, BF16),
        in_specs=[SCALARS, IN_PLACE],
        out_specs=IN_PLACE,
        scratch_shapes=[
            pltpu.VMEM((wet_dev,) + tile_shape, BF16),
            pltpu.SemaphoreType.DMA((wet_dev,)),
            pltpu.SemaphoreType.DMA((wet_dev,)),
        ],
        name="slot_order",
    )(source_chip, arrived)


def solution(mesh):
    return jax.shard_map(
        on_device,
        mesh=mesh,
        in_specs=(
            P("row", "col", None, None, None),
            P("row", "col"),
            P("row", "col", None),
            P(("row", "col")),
            P(),
            P(),
            P(),
            P(),
            P(),
        ),
        out_specs=P(("row", "col"), None, None, None),
        check_vma=False,
    )
```

profile of v0, /device:TPU:92, one launch (start us, length us, event | category | flops | bytes accessed | tf_op | source)
XLA Modules:
  0.0 172.5 jit_solution(5615440780295428931)
XLA Ops:
  0.0 1.4 fusion.11
  1.4 1.2 broadcast_in_dim.33
  2.6 7.3 %all-to-all-start = ((s32[32,1,1]{2,1,0:T(1,128)}), s32[32,1,1]{2,1,0:T(1,128)S(1)}, u32[]{:S(2)}, u32[]{:S(2)}) async-start(s32[32,1,1]{2,1,0:T(1,128)} %broadcast_in_dim.33), calls=%async_computation | async-start | bytes 32768 | tf_op jit(solution)/shard_map/all_to_all | solution.py:290
  10.0 0.1 mul.66
  10.1 0.9 fusion.6
  11.0 0.1 bitcast_multiply_fusion.1
  11.1 3.5 %collective-permute-start = (bf16[256,128]{1,0:T(8,128)(2,1)S(1)}, bf16[256,128]{1,0:T(8,128)(2,1)S(1)}, u32[]{:S(2)}, u32[]{:S(2)}) collective-permute-start(bf16[256,128]{1,0:T(8,128)(2,1)S(1)} %bitcast_multiply_fusion.1), channel_id=1, source_target_pairs={{0,32},{32,64},{64,96},{1,33},{33,65},{65,97},{2,34},{34,66},{66,9... | collective-permute-start | bytes 196616 | tf_op jit(solution)/shard_map/ppermute | solution.py:264
  14.7 0.1 mul.71
  14.8 0.1 bitcast_multiply_fusion
  14.9 2.3 %collective-permute-start.1 = (bf16[256,128]{1,0:T(8,128)(2,1)S(1)}, bf16[256,128]{1,0:T(8,128)(2,1)S(1)}, u32[]{:S(2)}, u32[]{:S(2)}) collective-permute-start(bf16[256,128]{1,0:T(8,128)(2,1)S(1)} %bitcast_multiply_fusion), channel_id=1, source_target_pairs={{32,0},{64,32},{96,64},{33,1},{65,33},{97,65},{34,2},{66,34},{98,6... | collective-permute-start | bytes 196616 | tf_op jit(solution)/shard_map/ppermute | solution.py:264
  17.2 0.8 reshape.27.wet_ref
  18.0 0.2 slice_reduce_fusion.2
  18.2 1.0 fusion.5
  19.2 1.0 slice_reduce_fusion.1
  20.2 0.1 mul.81
  20.4 0.1 mul.76
  20.7 0.1 select_reduce_fusion
  20.8 0.3 collective-permute-done.1.south_ref
  21.1 1.9 %collective-permute-start.2 = (bf16[66,128]{1,0:T(8,128)(2,1)S(1)}, bf16[66,128]{1,0:T(8,128)(2,1)S(1)}, u32[]{:S(2)}, u32[]{:S(2)}) collective-permute-start(bf16[66,128]{1,0:T(8,128)(2,1)S(1)} %pad_maximum_fusion), channel_id=1, source_target_pairs={{0,1},{1,2},{2,3},{3,4},{4,5},{5,6},{6,7},{7,8},{8,9},{9,10},{10,1... | collective-permute-start | bytes 50696 | tf_op jit(solution)/shard_map/ppermute | solution.py:264
  23.0 3.6 %collective-permute-start.3 = (bf16[66,128]{1,0:T(8,128)(2,1)S(1)}, bf16[66,128]{1,0:T(8,128)(2,1)S(1)}, u32[]{:S(2)}, u32[]{:S(2)}) collective-permute-start(bf16[66,128]{1,0:T(8,128)(2,1)S(1)} %pad_maximum_fusion.1), channel_id=1, source_target_pairs={{1,0},{2,1},{3,2},{4,3},{5,4},{6,5},{7,6},{8,7},{9,8},{10,9},{11,1... | collective-permute-start | bytes 50696 | tf_op jit(solution)/shard_map/ppermute | solution.py:264
  26.7 0.1 copy.21
  26.8 0.7 reshape.28.flag_ref
  27.5 0.7 reduce.1
  28.2 0.5 copy-done.5
  28.8 13.6 %first_conv.1 = (bf16[64,256,128]{2,1,0:T(8,128)(2,1)}, bf16[64,128]{1,0:T(8,128)(2,1)}, bf16[64,128]{1,0:T(8,128)(2,1)}) custom-call(s32[16]{0:T(128)} %copy-done.9, s32[4]{0:T(128)} %reshape.28.flag_ref, bf16[2,8,32,32,128]{4,3,2,1,0:T(8,128)(2,1)} %fields_ref.3, bf16[256,128]{1,0:T(8,128)(2,1)} %copy-done.1, bf16[256,128]{1,0:T(8,128)(2,1)} %copy-done.2, ...), custom_call_target="tpu_custom_call" | custom-call | tf_op jit(solution)/shard_map/first_conv/pallas_call | solution.py:312
  42.4 0.9 slice_bitcast_fusion
  43.3 2.3 %collective-permute-start.5 = (bf16[256,128]{1,0:T(8,128)(2,1)S(1)}, bf16[256,128]{1,0:T(8,128)(2,1)S(1)}, u32[]{:S(2)}, u32[]{:S(2)}) collective-permute-start(bf16[256,128]{1,0:T(8,128)(2,1)S(1)} %get-tuple-element.22), channel_id=1, source_target_pairs={{32,0},{64,32},{96,64},{33,1},{65,33},{97,65},{34,2},{66,34},{98,6... | collective-permute-start | bytes 196616 | tf_op jit(solution)/shard_map/ppermute | solution.py:264
  45.6 0.7 fusion.2
  46.3 3.5 %collective-permute-start.4 = (bf16[256,128]{1,0:T(8,128)(2,1)S(1)}, bf16[256,128]{1,0:T(8,128)(2,1)S(1)}, u32[]{:S(2)}, u32[]{:S(2)}) collective-permute-start(bf16[256,128]{1,0:T(8,128)(2,1)S(1)} %get-tuple-element.23), channel_id=1, source_target_pairs={{0,32},{32,64},{64,96},{1,33},{33,65},{65,97},{2,34},{34,66},{66,9... | collective-permute-start | bytes 196616 | tf_op jit(solution)/shard_map/ppermute | solution.py:264
  49.9 2.6 %collective-permute-done.4.north_ref = bf16[256,128]{1,0:T(8,128)(2,1)S(1)} collective-permute-done((bf16[256,128]{1,0:T(8,128)(2,1)S(1)}, bf16[256,128]{1,0:T(8,128)(2,1)S(1)}, u32[]{:S(2)}, u32[]{:S(2)}) %collective-permute-start.4) | collective-permute-done | bytes 65568 | tf_op jit(solution)/shard_map/ppermute | solution.py:264
  52.4 0.8 pad_maximum_fusion.2
  53.2 3.8 %collective-permute-start.6 = (bf16[66,128]{1,0:T(8,128)(2,1)S(1)}, bf16[66,128]{1,0:T(8,128)(2,1)S(1)}, u32[]{:S(2)}, u32[]{:S(2)}) collective-permute-start(bf16[66,128]{1,0:T(8,128)(2,1)S(1)} %pad_maximum_fusion.2), channel_id=1, source_target_pairs={{0,1},{1,2},{2,3},{3,4},{4,5},{5,6},{6,7},{7,8},{8,9},{9,10},{10,1... | collective-permute-start | bytes 50696 | tf_op jit(solution)/shard_map/ppermute | solution.py:264
  57.0 0.7 pad_maximum_fusion.3
  57.8 2.1 %collective-permute-start.7 = (bf16[66,128]{1,0:T(8,128)(2,1)S(1)}, bf16[66,128]{1,0:T(8,128)(2,1)S(1)}, u32[]{:S(2)}, u32[]{:S(2)}) collective-permute-start(bf16[66,128]{1,0:T(8,128)(2,1)S(1)} %pad_maximum_fusion.3), channel_id=1, source_target_pairs={{1,0},{2,1},{3,2},{4,3},{5,4},{6,5},{7,6},{8,7},{9,8},{10,9},{11,1... | collective-permute-start | bytes 50696 | tf_op jit(solution)/shard_map/ppermute | solution.py:264
  59.9 1.8 %compare_select_fusion.6.dst_ref = s32[16]{0:T(128)} fusion(s32[16]{0:T(128)} %copy-done.9, s32[16]{0:T(128)S(1)} %select_reduce_fusion, s32[]{:T(128)S(6)} %select_n.75, s32[]{:T(128)} %get-tuple-element.19), kind=kLoop, calls=%fused_computation.22 | loop fusion | flops 880 | bytes 200 | tf_op jit(solution)/shard_map/jit(_where)/select_n | solution.py:300
  61.7 0.2 collective-permute-done.7.east_ref
  61.8 0.4 copy-done.7
  62.3 0.2 copy-done.8
  62.4 18.7 %second_conv.1 = (bf16[16,32,32,128]{3,2,1,0:T(8,128)(2,1)}, bf16[8,32,32,128]{3,2,1,0:T(8,128)(2,1)}) custom-call(s32[16]{0:T(128)} %compare_select_fusion.6.dst_ref, s32[4]{0:T(128)} %reshape.28.flag_ref, bf16[64,256,128]{2,1,0:T(8,128)(2,1)} %get-tuple-element.10.hid_hbm, bf16[2,8,32,32,128]{4,3,2,1,0:T(8,128)(2,1)} %fields_ref.3, ...), custom_call_target="tpu_custom_call" | custom-call | tf_op jit(solution)/shard_map/second_conv/pallas_call | solution.py:340
  81.2 5.8 %collective-permute-start.8 = (bf16[8,32,32,128]{3,2,1,0:T(8,128)(2,1)}, bf16[8,32,32,128]{3,2,1,0:T(8,128)(2,1)S(1)}, u32[]{:S(2)}, u32[]{:S(2)}) collective-permute-start(bf16[8,32,32,128]{3,2,1,0:T(8,128)(2,1)} %get-tuple-element.13), channel_id=1, source_target_pairs={{0,1},{1,0},{2,3},{3,2},{4,5},{5,4},{6,7},{7,6},{8,9},{9,8},{10,11... | collective-permute-start | bytes 6291464 | tf_op jit(solution)/shard_map/ppermute | solution.py:367
  87.5 1.8 %compare_select_fusion.7.dst_ref = s32[8]{0:T(128)} fusion(s32[]{:T(128)} %get-tuple-element.21, s32[]{:T(128)} %get-tuple-element.20, s32[]{:T(128)S(6)} %select_n.76), kind=kLoop, calls=%fused_computation.25 | loop fusion | flops 248 | bytes 44 | tf_op jit(solution)/shard_map/jit(_where)/select_n | solution.py:303
  89.3 1.6 collective-permute-done.8.src_ref
  91.0 1.3 copy-done
  92.3 2.8 %merge_mate.1 = bf16[16,32,32,128]{3,2,1,0:T(8,128)(2,1)} custom-call(s32[8]{0:T(128)} %compare_select_fusion.7.dst_ref, bf16[8,32,32,128]{3,2,1,0:T(8,128)(2,1)} %copy-done, bf16[16,32,32,128]{3,2,1,0:T(8,128)(2,1)} %get-tuple-element.14.held_ref), custom_call_target="tpu_custom_call", output_to_operand_aliasing={{}: (2, {})} | custom-call | tf_op jit(solution)/shard_map/merge_mate/pallas_call | solution.py:368
  95.1 6.9 %all-to-all-start.1 = ((bf16[16,32,32,128]{3,2,1,0:T(8,128)(2,1)}), bf16[16,32,32,128]{3,2,1,0:T(8,128)(2,1)}, u32[]{:S(2)}, u32[]{:S(2)}) async-start(bf16[16,32,32,128]{3,2,1,0:T(8,128)(2,1)} %merge_mate.1), calls=%async_computation.1 | async-start | bytes 8388608 | tf_op jit(solution)/shard_map/all_to_all | solution.py:382
  102.1 0.6 and_select_fusion.6.idx_ref
  102.7 66.6 %all-to-all-done.1.src_ref = bf16[16,32,32,128]{3,2,1,0:T(8,128)(2,1)} async-done(((bf16[16,32,32,128]{3,2,1,0:T(8,128)(2,1)}), bf16[16,32,32,128]{3,2,1,0:T(8,128)(2,1)}, u32[]{:S(2)}, u32[]{:S(2)}) %all-to-all-start.1) | async-done | bytes 4194336 | tf_op jit(solution)/shard_map/all_to_all | solution.py:382
  169.3 3.1 %slot_order.1 = bf16[8,32,32,128]{3,2,1,0:T(8,128)(2,1)} custom-call(s32[8]{0:T(128)} %and_select_fusion.6.idx_ref, bf16[16,32,32,128]{3,2,1,0:T(8,128)(2,1)} %all-to-all-done.1.src_ref), custom_call_target="tpu_custom_call" | custom-call | tf_op jit(solution)/shard_map/slot_order/pallas_call | solution.py:385
  (40 shorter events, 0.6 us)
Async XLA Ops:
  2.6 24.8 %all-to-all-start = ((s32[32,1,1]{2,1,0:T(1,128)}), s32[32,1,1]{2,1,0:T(1,128)S(1)}, u32[]{:S(2)}, u32[]{:S(2)}) async-start(s32[32,1,1]{2,1,0:T(1,128)} %broadcast_in_dim.33), calls=%async_computation | async-start | bytes 32768 | tf_op jit(solution)/shard_map/all_to_all | solution.py:290
  11.1 9.7 %collective-permute-start = (bf16[256,128]{1,0:T(8,128)(2,1)S(1)}, bf16[256,128]{1,0:T(8,128)(2,1)S(1)}, u32[]{:S(2)}, u32[]{:S(2)}) collective-permute-start(bf16[256,128]{1,0:T(8,128)(2,1)S(1)} %bitcast_multiply_fusion.1), channel_id=1, source_target_pairs={{0,32},{32,64},{64,96},{1,33},{33,65},{65,97},{2,34},{34,66},{66,9... | collective-permute-start | bytes 196616 | tf_op jit(solution)/shard_map/ppermute | solution.py:264
  14.9 6.2 %collective-permute-start.1 = (bf16[256,128]{1,0:T(8,128)(2,1)S(1)}, bf16[256,128]{1,0:T(8,128)(2,1)S(1)}, u32[]{:S(2)}, u32[]{:S(2)}) collective-permute-start(bf16[256,128]{1,0:T(8,128)(2,1)S(1)} %bitcast_multiply_fusion), channel_id=1, source_target_pairs={{32,0},{64,32},{96,64},{33,1},{65,33},{97,65},{34,2},{66,34},{98,6... | collective-permute-start | bytes 196616 | tf_op jit(solution)/shard_map/ppermute | solution.py:264
  18.0 10.2 %copy-start.9 = (s32[16]{0:T(128)}, s32[16]{0:T(128)S(1)}, u32[]{:S(2)}) copy-start(s32[16]{0:T(128)S(1)} %reshape.27.wet_ref) | copy-start | bytes 196
  20.8 7.4 %copy-start.1 = (bf16[256,128]{1,0:T(8,128)(2,1)}, bf16[256,128]{1,0:T(8,128)(2,1)S(1)}, u32[]{:S(2)}) copy-start(bf16[256,128]{1,0:T(8,128)(2,1)S(1)} %collective-permute-done.north_ref) | copy-start | bytes 196612
  21.1 7.1 %copy-start.2 = (bf16[256,128]{1,0:T(8,128)(2,1)}, bf16[256,128]{1,0:T(8,128)(2,1)S(1)}, u32[]{:S(2)}) copy-start(bf16[256,128]{1,0:T(8,128)(2,1)S(1)} %collective-permute-done.1.south_ref) | copy-start | bytes 196612
  21.1 7.0 %collective-permute-start.2 = (bf16[66,128]{1,0:T(8,128)(2,1)S(1)}, bf16[66,128]{1,0:T(8,128)(2,1)S(1)}, u32[]{:S(2)}, u32[]{:S(2)}) collective-permute-start(bf16[66,128]{1,0:T(8,128)(2,1)S(1)} %pad_maximum_fusion), channel_id=1, source_target_pairs={{0,1},{1,2},{2,3},{3,4},{4,5},{5,6},{6,7},{7,8},{8,9},{9,10},{10,1... | collective-permute-start | bytes 50696 | tf_op jit(solution)/shard_map/ppermute | solution.py:264
  23.0 5.1 %collective-permute-start.3 = (bf16[66,128]{1,0:T(8,128)(2,1)S(1)}, bf16[66,128]{1,0:T(8,128)(2,1)S(1)}, u32[]{:S(2)}, u32[]{:S(2)}) collective-permute-start(bf16[66,128]{1,0:T(8,128)(2,1)S(1)} %pad_maximum_fusion.1), channel_id=1, source_target_pairs={{1,0},{2,1},{3,2},{4,3},{5,4},{6,5},{7,6},{8,7},{9,8},{10,9},{11,1... | collective-permute-start | bytes 50696 | tf_op jit(solution)/shard_map/ppermute | solution.py:264
  28.1 0.6 copy-start.5
  28.2 0.6 copy-start.6
  43.3 6.6 %collective-permute-start.5 = (bf16[256,128]{1,0:T(8,128)(2,1)S(1)}, bf16[256,128]{1,0:T(8,128)(2,1)S(1)}, u32[]{:S(2)}, u32[]{:S(2)}) collective-permute-start(bf16[256,128]{1,0:T(8,128)(2,1)S(1)} %get-tuple-element.22), channel_id=1, source_target_pairs={{32,0},{64,32},{96,64},{33,1},{65,33},{97,65},{34,2},{66,34},{98,6... | collective-permute-start | bytes 196616 | tf_op jit(solution)/shard_map/ppermute | solution.py:264
  46.3 6.1 %collective-permute-start.4 = (bf16[256,128]{1,0:T(8,128)(2,1)S(1)}, bf16[256,128]{1,0:T(8,128)(2,1)S(1)}, u32[]{:S(2)}, u32[]{:S(2)}) collective-permute-start(bf16[256,128]{1,0:T(8,128)(2,1)S(1)} %get-tuple-element.23), channel_id=1, source_target_pairs={{0,32},{32,64},{64,96},{1,33},{33,65},{65,97},{2,34},{34,66},{66,9... | collective-permute-start | bytes 196616 | tf_op jit(solution)/shard_map/ppermute | solution.py:264
  49.8 12.0 %copy-start.3 = (bf16[256,128]{1,0:T(8,128)(2,1)}, bf16[256,128]{1,0:T(8,128)(2,1)S(1)}, u32[]{:S(2)}) copy-start(bf16[256,128]{1,0:T(8,128)(2,1)S(1)} %collective-permute-done.5.south_ref) | copy-start | bytes 196612
  52.4 9.4 %copy-start.4 = (bf16[256,128]{1,0:T(8,128)(2,1)}, bf16[256,128]{1,0:T(8,128)(2,1)S(1)}, u32[]{:S(2)}) copy-start(bf16[256,128]{1,0:T(8,128)(2,1)S(1)} %collective-permute-done.4.north_ref) | copy-start | bytes 196612
  53.2 8.5 %collective-permute-start.6 = (bf16[66,128]{1,0:T(8,128)(2,1)S(1)}, bf16[66,128]{1,0:T(8,128)(2,1)S(1)}, u32[]{:S(2)}, u32[]{:S(2)}) collective-permute-start(bf16[66,128]{1,0:T(8,128)(2,1)S(1)} %pad_maximum_fusion.2), channel_id=1, source_target_pairs={{0,1},{1,2},{2,3},{3,4},{4,5},{5,6},{6,7},{7,8},{8,9},{9,10},{10,1... | collective-permute-start | bytes 50696 | tf_op jit(solution)/shard_map/ppermute | solution.py:264
  57.8 4.1 %collective-permute-start.7 = (bf16[66,128]{1,0:T(8,128)(2,1)S(1)}, bf16[66,128]{1,0:T(8,128)(2,1)S(1)}, u32[]{:S(2)}, u32[]{:S(2)}) collective-permute-start(bf16[66,128]{1,0:T(8,128)(2,1)S(1)} %pad_maximum_fusion.3), channel_id=1, source_target_pairs={{1,0},{2,1},{3,2},{4,3},{5,4},{6,5},{7,6},{8,7},{9,8},{10,9},{11,1... | collective-permute-start | bytes 50696 | tf_op jit(solution)/shard_map/ppermute | solution.py:264
  61.7 0.6 copy-start.7
  61.8 0.6 copy-start.8
  81.2 9.8 %collective-permute-start.8 = (bf16[8,32,32,128]{3,2,1,0:T(8,128)(2,1)}, bf16[8,32,32,128]{3,2,1,0:T(8,128)(2,1)S(1)}, u32[]{:S(2)}, u32[]{:S(2)}) collective-permute-start(bf16[8,32,32,128]{3,2,1,0:T(8,128)(2,1)} %get-tuple-element.13), channel_id=1, source_target_pairs={{0,1},{1,0},{2,3},{3,2},{4,5},{5,4},{6,7},{7,6},{8,9},{9,8},{10,11... | collective-permute-start | bytes 6291464 | tf_op jit(solution)/shard_map/ppermute | solution.py:367
  91.0 1.3 copy-start
  95.1 7.0 %copy-start.10 = (s32[8]{0:T(128)S(1)}, s32[8]{0:T(128)}, u32[]{:S(2)}) copy-start(s32[8]{0:T(128)} %param.12) | copy-start | bytes 100
  95.1 74.1 %all-to-all-start.1 = ((bf16[16,32,32,128]{3,2,1,0:T(8,128)(2,1)}), bf16[16,32,32,128]{3,2,1,0:T(8,128)(2,1)}, u32[]{:S(2)}, u32[]{:S(2)}) async-start(bf16[16,32,32,128]{3,2,1,0:T(8,128)(2,1)} %merge_mate.1), calls=%async_computation.1 | async-start | bytes 8388608 | tf_op jit(solution)/shard_map/all_to_all | solution.py:382
where the time goes:
time: 174 us; the launch traced here: 172 us
  waiting for transfers between devices  71.2 us (41%)
  starting transfers between devices  43.2 us (25%)
  Pallas kernels  38.2 us (22%)
  local copies, waits for them, and re-layouts  9.88 us (6%)
  other arithmetic  8.89 us (5%)
    all_to_all x1, waiting for transfers between devices, on_device(): lax.all_to_all(sending, 'col', split_axis=0, concat_axis=0, tiled=True, a...  66.6 us
    ppermute x8, starting transfers between devices, shifted(): return lax.ppermute(x, axis, pairs)  23.2 us
    pallas_call x1, Pallas kernels, on_device(): pl.pallas_call(second_kernel, out_shape=(jax.ShapeDtypeStruct((chips,) +...  18.7 us
    pallas_call x1, Pallas kernels, on_device(): pl.pallas_call(first_kernel, out_shape=(jax.ShapeDtypeStruct((height, wid...  13.6 us
    all_to_all x1, starting transfers between devices, on_device(): lax.all_to_all(total, 'col', split_axis=0, concat_axis=0, tiled=True)  7.28 us
    all_to_all x1, starting transfers between devices, on_device(): lax.all_to_all(sending, 'col', split_axis=0, concat_axis=0, tiled=True, a...  6.94 us
    ppermute x1, starting transfers between devices, on_device(): taken = lax.ppermute(give, 'col', [(i, i ^ 1) for i in range(columns)])  5.78 us
  transfers between devices with their start and end apart: 11, of which 5 were waited for; matrix products, arithmetic and copies ran while one was open for 7% of the time, Pallas kernels for 0%

commit v1 on v0

v1 whole, which is shorter than its diff:
```python
import functools

import jax
import jax.numpy as jnp
from jax import lax
from jax.experimental import pallas as pl
from jax.experimental.pallas import tpu as pltpu
from jax.sharding import PartitionSpec as P

F32 = jnp.float32
BF16 = jnp.bfloat16
VMEM_LIMIT = 56 * 1024 * 1024
WHOLE = pl.BlockSpec(memory_space=pltpu.VMEM)
SCALARS = pl.BlockSpec(memory_space=pltpu.SMEM)
IN_PLACE = pl.BlockSpec(memory_space=pl.ANY)


def dot(a, b):
    return jnp.dot(a, b, preferred_element_type=F32)


def gelu(x):
    u = x * (0.7978845608028654 + 0.03567740813636141 * (x * x))
    half = 0.5 * x
    return half + half * jnp.tanh(u)


def fill_weights(k_ref, w_ref):
    ch = k_ref.shape[2]
    zero = jnp.zeros((ch, 3 * ch), BF16)
    w_ref[3 * ch :, : 3 * ch] = zero
    w_ref[:ch, 3 * ch :] = zero
    for dy in range(3):
        for dx in range(3):
            block = k_ref[dy, dx]
            w_ref[dy * ch : (dy + 1) * ch, dx * ch : (dx + 1) * ch] = block
            w_ref[(dy + 1) * ch : (dy + 2) * ch, (3 + dx) * ch : (4 + dx) * ch] = block


def tall_conv(t_ref, k_ref, dx, count):
    total = dot(t_ref[0:count].astype(BF16), k_ref[0, dx])
    total += dot(t_ref[1 : count + 1].astype(BF16), k_ref[1, dx])
    total += dot(t_ref[2 : count + 2].astype(BF16), k_ref[2, dx])
    return total


def put_columns(t_ref, col_ref, base, tr_dev, tile):
    tall = tile + 2
    t_ref[0:3] = col_ref[base : base + 3]
    for i in range(tr_dev):
        t_ref[3 + tall * i : 3 + tall * (i + 1)] = col_ref[
            base + 1 + tile * i : base + 1 + tile * i + tall
        ]
    last = 3 + tall * tr_dev
    t_ref[last : last + 3] = col_ref[base + 1 + tile * tr_dev : base + 4 + tile * tr_dev]


def put_pads(t_ref, above, ext_ref, base, flags, below, flip, tile):
    tall = tile + 2
    for n, line in enumerate(above):
        t_ref[n : n + 1] = line
    for i, flag in enumerate(flags):
        at = 3 + tall * i
        from_row = base + tile * i
        t_ref[at : at + 1] = ext_ref[from_row : from_row + 1]
        middle = ext_ref[from_row + 1 : from_row + 1 + tile]
        turned = dot(flip, middle.astype(BF16))
        t_ref[at + 1 : at + 1 + tile] = jnp.where(flag == 1, turned, middle)
        t_ref[at + tall - 1 : at + tall] = ext_ref[from_row + tile + 1 : from_row + tile + 2]
    last = 3 + tall * len(flags)
    for n, line in enumerate(below):
        t_ref[last + n : last + n + 1] = line


def line_at(tall_row, tile):
    return 3 + tall_row + 2 * (tall_row // tile)


def side_sums(z, taps, west, east):
    ch = west.shape[1]
    width = z.shape[0]
    lane_row = lax.broadcasted_iota(jnp.int32, (8, ch), 0)
    left = pltpu.roll(z[:, taps : taps + ch], 1, 0)
    right = pltpu.roll(z[:, taps + 2 * ch : taps + 3 * ch], width - 1, 0)
    left = jnp.concatenate([jnp.where(lane_row == 0, west, left[:8]), left[8:]], axis=0)
    right = jnp.concatenate(
        [right[: width - 8], jnp.where(lane_row == 7, east, right[width - 8 :])], axis=0
    )
    return z[:, taps + ch : taps + 2 * ch] + left + right


def conv_pair(window, w_ref, bias, zw_ref, ze_ref, line):
    ch = window[0].shape[1]
    z = dot(jnp.concatenate(window, axis=1), w_ref[...])
    outs = []
    for ro in range(2):
        west = zw_ref[pl.ds(line + ro, 1), :]
        east = ze_ref[pl.ds(line + ro, 1), :]
        outs.append(side_sums(z, 3 * ro * ch, west, east) + bias)
    return outs


def rim_kernel(
    wet_ref, flag_ref, fields_ref, top_ref, bottom_ref, lcol_ref, rcol_ref,
    rows_ref, cols_ref, line_ref, sems,
):
    tr_dev, tc_dev, tile, _, ch = fields_ref.shape
    width, height = tc_dev * tile, tr_dev * tile
    part = cols_ref.shape[3]
    loads = [
        pltpu.make_async_copy(fields_ref.at[0, :, 0:2], rows_ref.at[0], sems.at[0]),
        pltpu.make_async_copy(fields_ref.at[tr_dev - 1, :, tile - 2 : tile], rows_ref.at[1], sems.at[1]),
        pltpu.make_async_copy(fields_ref.at[:, 0, :, 0:part], cols_ref.at[0], sems.at[2]),
        pltpu.make_async_copy(fields_ref.at[:, tc_dev - 1, :, tile - part :], cols_ref.at[1], sems.at[3]),
    ]
    for load in loads:
        load.start()
    for load in loads:
        load.wait()

    def wet(i, j):
        return jnp.full((1, ch), 1.0, F32) * wet_ref[i * tc_dev + j].astype(F32)

    for side, (out_ref, i) in enumerate(((top_ref, 0), (bottom_ref, tr_dev - 1))):
        for j in range(tc_dev):
            scale = wet(i, j).astype(BF16)
            for n in range(2):
                out_ref[n * width + j * tile : n * width + (j + 1) * tile] = (
                    rows_ref[side, j, n] * scale
                )
    picked = []
    for side, out_ref in enumerate((lcol_ref, rcol_ref)):
        for i in range(tr_dev):
            block = cols_ref[side, i].astype(F32) * wet(i, side * (tc_dev - 1))[None]
            line_ref[side, i * tile * part : (i + 1) * tile * part] = block.reshape(tile * part, ch)
        first = side * (part - 2)
        columns = [line_ref[side, pl.ds(first + n, height, stride=part)] for n in range(2)]
        out_ref[0] = columns[0].astype(BF16)
        out_ref[1] = columns[1].astype(BF16)
        picked.append(columns[side])
    for out_ref, i, near in ((top_ref, 0, tile - 2), (bottom_ref, tr_dev - 1, tile * (tr_dev - 1))):
        flags = [jnp.full((1, ch), 1.0, F32) * flag_ref[2 * i + side].astype(F32) for side in range(2)]
        extra = [column[near : near + 2] for column in picked]
        extra += [wet(i, j) for j in range(tc_dev)] + flags
        extra.append(jnp.zeros((12 - tc_dev - 2, ch), F32))
        at = 0
        for piece in extra:
            line_ref[0, at : at + piece.shape[0]] = piece
            at += piece.shape[0]
        out_ref[2 * width : 2 * width + 16] = line_ref[0, 0:16].astype(BF16)


def conv_kernel(
    wet_ref, flag_ref, dst_ref, fields_ref, north_ref, south_ref, west_ref, east_ref,
    lcol_ref, rcol_ref, k1_ref, b1_ref, k2_ref, b2_ref, mix_ref, keep_ref, give_ref,
    out_ref, x_ref, hid_ref, w1_ref, w2_ref, mm_ref, m_ref, pack_ref, own_ref, ext_ref, t_ref,
    zw1_ref, ze1_ref, zw2_ref, ze2_ref, in_sems, sems,
):
    tr_dev, tc_dev, tile, _, ch = fields_ref.shape
    width, height = tc_dev * tile, tr_dev * tile
    slots = keep_ref.shape[0]
    tall = 3 + (tile + 2) * tr_dev + 3
    lines = tall - 2
    loads = [
        pltpu.make_async_copy(fields_ref.at[i], out_ref.at[i], in_sems.at[i]) for i in range(tr_dev)
    ]
    for load in loads:
        load.start()
    fill_weights(k1_ref, w1_ref)
    fill_weights(k2_ref, w2_ref)
    zero = jnp.zeros((ch, ch), BF16)
    mm_ref[:ch, :ch] = mix_ref[...]
    mm_ref[ch:, ch:] = mix_ref[...]
    mm_ref[:ch, ch:] = zero
    mm_ref[ch:, :ch] = zero
    bias1 = b1_ref[...]
    bias2 = b2_ref[...]
    rows = lax.broadcasted_iota(jnp.int32, (tile, tile), 0)
    cols = lax.broadcasted_iota(jnp.int32, (tile, tile), 1)
    flip = jnp.where(rows + cols == tile - 1, 1.0, 0.0).astype(BF16)

    notes = [ref[2 * width : 2 * width + 16].astype(F32) for ref in (north_ref, south_ref)]
    flagged = [[note[4 + tc_dev + s : 5 + tc_dev + s] > 0.5 for s in range(2)] for note in notes]

    def pixel(ref, n):
        base = n // 16 * 16
        return ref[base : base + 16].astype(F32)[n - base : n - base + 1]

    step_size = pack_ref.shape[1] // 20 * 9
    sides = ((west_ref, lcol_ref, 0), (east_ref, rcol_ref, width - 1))
    for s, (pack, own, c) in enumerate(sides):
        pack_ref[s] = pack[...].astype(F32)
        own_ref[s, 1 : height + 1] = own[...].astype(F32)
        own_ref[s, 0:1] = pixel(north_ref, width + c)
        own_ref[s, height + 1 : height + 2] = pixel(south_ref, c)
    for s, (pack, own, c) in enumerate(sides):
        near = step_size * (1 - s)
        far = step_size * s
        notes_at = 2 * step_size
        note = [pack_ref[s, notes_at + n : notes_at + n + 1] for n in range(8)]
        held = pack_ref.at[s]
        mine = own_ref.at[s]
        flags = [flag_ref[2 * i + s] for i in range(tr_dev)]
        north_flag, south_flag = flagged[0][s], flagged[1][s]

        def near_line(n, near=near, held=held):
            return held[near + n : near + n + 1]

        above = [
            jnp.where(north_flag, note[1], near_line(0)),
            jnp.where(north_flag, note[0], near_line(1)),
            near_line(2),
        ]
        below = [
            near_line(height + 1),
            jnp.where(south_flag, note[3], near_line(height + 2)),
            jnp.where(south_flag, note[2], near_line(height + 3)),
        ]
        put_pads(t_ref.at[0], above, held, near + 1, flags, below, flip, tile)
        z_ref = (zw1_ref, ze1_ref)[s]
        z_ref[0:lines] = tall_conv(t_ref.at[0], k1_ref, 2 * s, lines)
        total = bias1
        put_columns(t_ref.at[1], held, near, tr_dev, tile)
        total = total + tall_conv(t_ref.at[1], k1_ref, 1, lines)
        put_columns(t_ref.at[2], held, far, tr_dev, tile)
        total = total + tall_conv(t_ref.at[2], k1_ref, 2 * s, lines)
        above = [
            jnp.where(north_flag, notes[0][2 * s + 1 : 2 * s + 2], pixel(north_ref, c)),
            jnp.where(north_flag, notes[0][2 * s : 2 * s + 1], pixel(north_ref, width + c)),
            mine[1:2],
        ]
        below = [
            mine[height : height + 1],
            jnp.where(south_flag, notes[1][2 * s + 1 : 2 * s + 2], pixel(south_ref, c)),
            jnp.where(south_flag, notes[1][2 * s : 2 * s + 1], pixel(south_ref, width + c)),
        ]
        put_pads(t_ref.at[3], above, mine, 0, flags, below, flip, tile)
        total = total + tall_conv(t_ref.at[3], k1_ref, 2 - 2 * s, lines)
        value = gelu(total)
        spare = ext_ref.at[s]
        spare[0:1] = value[0:1] * note[4 + tr_dev]
        for i in range(tr_dev):
            at = line_at(i * tile, tile)
            spare[1 + i * tile : 1 + (i + 1) * tile] = value[at : at + tile] * note[4 + i]
        spare[height + 1 : height + 2] = value[lines - 1 : lines] * note[5 + tr_dev]
        put_pads(t_ref.at[0], [], spare, 0, flags, [], flip, tile)
        z_ref = (zw2_ref, ze2_ref)[s]
        z_ref[0:lines] = tall_conv(t_ref.at[0], k2_ref, 2 * s, lines)

    x_ref[0] = north_ref[width : 2 * width]
    x_ref[height + 1] = south_ref[0:width]
    for i in range(tr_dev):
        loads[i].wait()
        for j in range(tc_dev):
            scale = jnp.full((1, ch), 1.0, F32) * wet_ref[i * tc_dev + j].astype(F32)
            m_ref[i, j * tile : (j + 1) * tile] = jnp.broadcast_to(scale, (tile, ch))
            x_ref[1 + i * tile : 1 + (i + 1) * tile, j * tile : (j + 1) * tile] = (
                out_ref[i, j] * scale.astype(BF16)[None]
            )

    beyond = (
        (0, [north_ref[0:width], north_ref[width : 2 * width], x_ref[1]], 0, notes[0]),
        (height + 1, [x_ref[height], south_ref[0:width], south_ref[width : 2 * width]], lines - 1, notes[1]),
    )
    for row, window, line, note in beyond:
        z = dot(jnp.concatenate(window, axis=1), w1_ref[: 3 * ch, : 3 * ch])
        total = side_sums(z, 0, zw1_ref[line : line + 1], ze1_ref[line : line + 1]) + bias1
        value = gelu(total)
        for j in range(tc_dev):
            hid_ref[row, j * tile : (j + 1) * tile] = (
                value[j * tile : (j + 1) * tile] * note[4 + j : 5 + j]
            ).astype(BF16)

    def first(p, carry):
        row = 2 * p
        window = [x_ref[row + k] for k in range(4)]
        outs = conv_pair(window, w1_ref, bias1, zw1_ref, ze1_ref, line_at(row, tile))
        for ro in range(2):
            hid_ref[1 + row + ro] = (gelu(outs[ro]) * m_ref[row // tile]).astype(BF16)
        return carry

    def second(p, carry):
        row = 2 * p
        i = row // tile
        inner = row % tile
        window = [hid_ref[row + k] for k in range(4)]
        outs = conv_pair(window, w2_ref, bias2, zw2_ref, ze2_ref, line_at(row, tile))
        branch = jnp.concatenate([gelu(o).astype(BF16) for o in outs], axis=1)
        mixed = dot(branch, mm_ref[...])
        for ro in range(2):
            own = out_ref[i, :, inner + ro].reshape(width, ch).astype(F32)
            total = (own + mixed[:, ro * ch : (ro + 1) * ch]).astype(BF16)
            out_ref[i, :, inner + ro] = total.reshape(tc_dev, tile, ch)
        return carry

    def copies(i, act):
        for j in range(tc_dev):
            k = i * tc_dev + j
            target = dst_ref[k]

            @pl.when((target >= 0) & (target < slots))
            def _():
                act(pltpu.make_async_copy(out_ref.at[i, j], keep_ref.at[target], sems.at[k]))

            @pl.when(target >= slots)
            def _():
                act(pltpu.make_async_copy(out_ref.at[i, j], give_ref.at[target - slots], sems.at[k]))

    lax.fori_loop(0, height // 2, first, 0, unroll=4)
    for i in range(tr_dev):
        lax.fori_loop(i * tile // 2, (i + 1) * tile // 2, second, 0, unroll=4)
        copies(i, lambda c: c.start())
    for i in range(tr_dev):
        copies(i, lambda c: c.wait())


def scatter_kernel(dst_ref, src_ref, held_ref, out_ref, buf_ref, in_sems, sems):
    def each(act):
        for k in range(src_ref.shape[0]):

            @pl.when(dst_ref[k] >= 0)
            def _():
                act(k)

    def load(k):
        return pltpu.make_async_copy(src_ref.at[k], buf_ref.at[k], in_sems.at[k])

    def store(k):
        return pltpu.make_async_copy(buf_ref.at[k], out_ref.at[dst_ref[k]], sems.at[k])

    def turn(k):
        load(k).wait()
        store(k).start()

    each(lambda k: load(k).start())
    each(turn)
    each(lambda k: store(k).wait())


def gather_kernel(idx_ref, src_ref, out_ref, buf_ref, in_sems, sems):
    count = out_ref.shape[0]

    def load(k):
        return pltpu.make_async_copy(src_ref.at[idx_ref[k]], buf_ref.at[k], in_sems.at[k])

    def store(k):
        return pltpu.make_async_copy(buf_ref.at[k], out_ref.at[k], sems.at[k])

    for k in range(count):
        load(k).start()
    for k in range(count):
        load(k).wait()
        store(k).start()
    for k in range(count):
        store(k).wait()


def shifted(x, axis, step):
    count = lax.axis_size(axis)
    pairs = [(i, i + step) for i in range(count) if 0 <= i + step < count]
    return lax.ppermute(x, axis, pairs)


def side_pack(north, south, columns, at, wets):
    width = (north.shape[0] - 16) // 2
    tc_dev = 8
    filler = jnp.zeros((4, north.shape[1]), north.dtype)
    pieces = []
    for n in range(2):
        c = at + n
        pieces += [north[c : c + 1], north[width + c : width + c + 1], columns[n]]
        pieces += [south[c : c + 1], south[width + c : width + c + 1], filler]
    side = 1 if at else 0
    tile = at and tc_dev - 1
    base = 2 * width
    pieces += [ref[base + 2 * side : base + 2 * side + 2] for ref in (north, south)]
    pieces += wets
    pieces += [ref[base + 4 + tile : base + 5 + tile] for ref in (north, south)]
    pieces.append(jnp.zeros((8, north.shape[1]), north.dtype))
    return jnp.concatenate(pieces, axis=0)


def on_device(
    fields, wet_mask, seam_flags, wet_list, kernel_one, bias_one, kernel_two, bias_two, mixing
):
    tr_dev, tc_dev, tile, _, ch = fields.shape
    face = tr_dev * tc_dev
    wet_dev = wet_list.shape[0]
    columns = lax.axis_size("col")
    chips = columns // 2
    width, height = tc_dev * tile, tr_dev * tile
    me = lax.axis_index("col")
    core = me % 2
    wet = wet_mask.reshape(face)
    flags = jnp.stack([seam_flags[:, 0, 0], seam_flags[:, tc_dev - 1, 1]], axis=1).reshape(-1)

    total = jnp.broadcast_to(jnp.sum(wet), (columns, 1, 1))
    counts = lax.all_to_all(total, "col", split_axis=0, concat_axis=0, tiled=True).reshape(columns)
    cids = jnp.arange(columns)
    start = jnp.sum(jnp.where(cids < me, counts, 0))
    mate = me ^ 1
    mate_start = jnp.sum(jnp.where(cids < mate, counts, 0))
    mate_count = jnp.sum(jnp.where(cids == mate, counts, 0))
    ids = jnp.arange(face)
    local = jnp.sum(jnp.where(ids[None, :] < ids[:, None], wet[None, :], 0), axis=1)
    rank = start + local
    slot = (rank % columns) // 2
    dst = jnp.where(wet == 1, jnp.where(rank % 2 == core, slot, chips + local // 2), -1)
    half = face // 2
    mate_local = 2 * jnp.arange(half) + (mate_start + core) % 2
    mate_dst = jnp.where(mate_local < mate_count, ((mate_start + mate_local) % columns) // 2, -1)
    source_chip = (wet_list % (tc_dev * columns)) // (2 * tc_dev)

    params = pltpu.CompilerParams(vmem_limit_bytes=VMEM_LIMIT)
    strip = jax.ShapeDtypeStruct((2 * width + 16, ch), BF16)
    pair = jax.ShapeDtypeStruct((2, height, ch), BF16)
    top, bottom, lcols, rcols = pl.pallas_call(
        rim_kernel,
        out_shape=(strip, strip, pair, pair),
        in_specs=[SCALARS, SCALARS, IN_PLACE],
        out_specs=(WHOLE,) * 4,
        scratch_shapes=[
            pltpu.VMEM((2, tc_dev, 2, tile, ch), BF16),
            pltpu.VMEM((2, tr_dev, tile, 16, ch), BF16),
            pltpu.VMEM((2, height * 16, ch), F32),
            pltpu.SemaphoreType.DMA((4,)),
        ],
        name="rim",
    )(wet, flags, fields)
    north = shifted(bottom, "row", 1)
    south = shifted(top, "row", -1)
    wets = jnp.broadcast_to(wet_mask.astype(BF16)[:, :, None, None], (tr_dev, tc_dev, 1, ch))
    west = shifted(
        side_pack(north, south, rcols, width - 2, [wets[i, -1] for i in range(tr_dev)]), "col", 1
    )
    east = shifted(side_pack(north, south, lcols, 0, [wets[i, 0] for i in range(tr_dev)]), "col", -1)

    tile_shape = (tile, tile, ch)
    lines = 8 + (tile + 2) * tr_dev
    lines += -lines % 8
    keep, give = pl.pallas_call(
        conv_kernel,
        out_shape=(
            jax.ShapeDtypeStruct((chips,) + tile_shape, BF16),
            jax.ShapeDtypeStruct((half,) + tile_shape, BF16),
        ),
        in_specs=[SCALARS] * 3 + [IN_PLACE] + [WHOLE] * 11,
        out_specs=(IN_PLACE, IN_PLACE),
        scratch_shapes=[
            pltpu.VMEM(fields.shape, BF16),
            pltpu.VMEM((height + 2, width, ch), BF16),
            pltpu.VMEM((height + 2, width, ch), BF16),
            pltpu.VMEM((4 * ch, 6 * ch), BF16),
            pltpu.VMEM((4 * ch, 6 * ch), BF16),
            pltpu.VMEM((2 * ch, 2 * ch), BF16),
            pltpu.VMEM((tr_dev, width, ch), F32),
            pltpu.VMEM((2,) + west.shape, F32),
            pltpu.VMEM((2, height + 8, ch), F32),
            pltpu.VMEM((2, height + 8, ch), F32),
            pltpu.VMEM((4, lines, ch), F32),
            pltpu.VMEM((lines, ch), F32),
            pltpu.VMEM((lines, ch), F32),
            pltpu.VMEM((lines, ch), F32),
            pltpu.VMEM((lines, ch), F32),
            pltpu.SemaphoreType.DMA((tr_dev,)),
            pltpu.SemaphoreType.DMA((face,)),
        ],
        compiler_params=params,
        name="both_convs",
    )(
        wet, flags, dst, fields, north, south, west, east, lcols[0], rcols[1],
        kernel_one, bias_one[None], kernel_two, bias_two[None], mixing,
    )

    taken = lax.ppermute(give, "col", [(i, i ^ 1) for i in range(columns)])
    sending = pl.pallas_call(
        scatter_kernel,
        out_shape=jax.ShapeDtypeStruct(keep.shape, BF16),
        in_specs=[SCALARS, IN_PLACE, IN_PLACE],
        out_specs=IN_PLACE,
        scratch_shapes=[
            pltpu.VMEM((half,) + tile_shape, BF16),
            pltpu.SemaphoreType.DMA((half,)),
            pltpu.SemaphoreType.DMA((half,)),
        ],
        input_output_aliases={2: 0},
        name="merge_mate",
    )(mate_dst, taken, keep)
    groups = [[2 * k + c for k in range(chips)] for c in range(2)]
    arrived = lax.all_to_all(
        sending, "col", split_axis=0, concat_axis=0, tiled=True, axis_index_groups=groups
    )
    return pl.pallas_call(
        gather_kernel,
        out_shape=jax.ShapeDtypeStruct((wet_dev,) + tile_shape, BF16),
        in_specs=[SCALARS, IN_PLACE],
        out_specs=IN_PLACE,
        scratch_shapes=[
            pltpu.VMEM((wet_dev,) + tile_shape, BF16),
            pltpu.SemaphoreType.DMA((wet_dev,)),
            pltpu.SemaphoreType.DMA((wet_dev,)),
        ],
        name="slot_order",
    )(source_chip, arrived)


def solution(mesh):
    return jax.shard_map(
        on_device,
        mesh=mesh,
        in_specs=(
            P("row", "col", None, None, None),
            P("row", "col"),
            P("row", "col", None),
            P(("row", "col")),
            P(),
            P(),
            P(),
            P(),
            P(),
        ),
        out_specs=P(("row", "col"), None, None, None),
        check_vma=False,
    )
```

time: 174 us -> 156 us (0.90)
  starting transfers between devices: 43.2 us -> 27.8 us
  other arithmetic: 8.89 us -> 5.7 us
  local copies, waits for them, and re-layouts: 9.88 us -> 11.8 us
    ppermute x8 -> x4, starting transfers between devices: 23.2 us -> 10.1 us  [shifted(): return lax.ppermute(x, axis, pairs)]
    ppermute x1, starting transfers between devices: 5.78 us -> 1.55 us  [on_device(): taken = lax.ppermute(give, 'col', [(i, i ^ 1) for i in range(columns)])]
    broadcast_in_dim x0 -> x4, local copies, waits for them, and re-layouts: none -> 2.57 us  [on_device(): jnp.broadcast_to(wet_mask.astype(BF16)[:, :, None, None], (tr_dev, tc_dev...]
    all_to_all x1, starting transfers between devices: 6.94 us -> 8.83 us  [on_device(): lax.all_to_all(sending, 'col', split_axis=0, concat_axis=0, tiled=True, a...]
  transfers between devices with their start and end apart: 11 -> 7, of which waited for: 5 -> 4; matrix products, arithmetic and copies ran while one was open for 7% -> 7% of each run, Pallas kernels for 0% -> 0%
where the time goes in v1:
time: 156 us; the launch traced here: 154 us
  waiting for transfers between devices  70.5 us (45%)
  Pallas kernels  37.3 us (24%)
  starting transfers between devices  27.8 us (18%)
  local copies, waits for them, and re-layouts  11.8 us (8%)
  other arithmetic  5.7 us (4%)
    all_to_all x1, waiting for transfers between devices, on_device(): lax.all_to_all(sending, 'col', split_axis=0, concat_axis=0, tiled=True, a...  65.7 us
    pallas_call x1, Pallas kernels, on_device(): pl.pallas_call(conv_kernel, out_shape=(jax.ShapeDtypeStruct((chips,) + ti...  28.8 us
    ppermute x4, starting transfers between devices, shifted(): return lax.ppermute(x, axis, pairs)  10.1 us
    all_to_all x1, starting transfers between devices, on_device(): lax.all_to_all(sending, 'col', split_axis=0, concat_axis=0, tiled=True, a...  8.83 us
    all_to_all x1, starting transfers between devices, on_device(): lax.all_to_all(total, 'col', split_axis=0, concat_axis=0, tiled=True)  7.28 us
  transfers between devices with their start and end apart: 7, of which 4 were waited for; matrix products, arithmetic and copies ran while one was open for 7% of the time, Pallas kernels for 0%

profile of v1, /device:TPU:92, one launch (start us, length us, event | category | flops | bytes accessed | tf_op | source)
XLA Modules:
  0.0 154.0 jit_solution(10021965326920994052)
XLA Ops:
  0.0 0.9 slice_reduce_fusion.1
  1.0 0.1 copy.15
  1.1 0.6 reshape.27.flag_ref
  1.7 1.3 reshape.26.wet_ref
  3.0 2.7 %rim.1 = (bf16[528,128]{1,0:T(8,128)(2,1)}, bf16[528,128]{1,0:T(8,128)(2,1)}, bf16[2,64,128]{2,1,0:T(8,128)(2,1)}, bf16[2,64,128]{2,1,0:T(8,128)(2,1)}) custom-call(s32[16]{0:T(128)} %reshape.26.wet_ref, s32[4]{0:T(128)} %reshape.27.flag_ref, bf16[2,8,32,32,128]{4,3,2,1,0:T(8,128)(2,1)} %fields_ref.3), custom_call_target="tpu_custom_call" | custom-call | tf_op jit(solution)/shard_map/rim/pallas_call | solution.py:417
  5.7 2.0 %collective-permute-start.1 = (bf16[528,128]{1,0:T(8,128)(2,1)}, bf16[528,128]{1,0:T(8,128)(2,1)S(1)}, u32[]{:S(2)}, u32[]{:S(2)}) collective-permute-start(bf16[528,128]{1,0:T(8,128)(2,1)} %get-tuple-element.12), channel_id=1, source_target_pairs={{32,0},{64,32},{96,64},{33,1},{65,33},{97,65},{34,2},{66,34},{98,6... | collective-permute-start | bytes 405512 | tf_op jit(solution)/shard_map/ppermute | solution.py:361
  7.7 3.8 %collective-permute-start = (bf16[528,128]{1,0:T(8,128)(2,1)}, bf16[528,128]{1,0:T(8,128)(2,1)S(1)}, u32[]{:S(2)}, u32[]{:S(2)}) collective-permute-start(bf16[528,128]{1,0:T(8,128)(2,1)} %get-tuple-element.11), channel_id=1, source_target_pairs={{0,32},{32,64},{64,96},{1,33},{33,65},{65,97},{2,34},{34,66},{66,9... | collective-permute-start | bytes 405512 | tf_op jit(solution)/shard_map/ppermute | solution.py:361
  11.6 0.0 copy-done.8
  11.6 0.6 fusion.9
  12.2 1.2 broadcast_in_dim.53
  13.5 7.3 %all-to-all-start = ((s32[32,1,1]{2,1,0:T(1,128)}), s32[32,1,1]{2,1,0:T(1,128)S(1)}, u32[]{:S(2)}, u32[]{:S(2)}) async-start(s32[32,1,1]{2,1,0:T(1,128)} %broadcast_in_dim.53), calls=%async_computation | async-start | bytes 32768 | tf_op jit(solution)/shard_map/all_to_all | solution.py:398
  20.8 0.0 copy-done.7
  20.8 0.1 select_reduce_fusion
  20.9 0.7 slice_bitcast_fusion
  21.6 0.7 slice_bitcast_fusion.2
  22.4 0.7 fusion.10
  23.0 1.5 all-to-all-done
  24.5 0.7 reduce.1
  25.2 0.7 fusion.2
  25.9 0.0 collective-permute-done.1.south_ref
  25.9 0.0 collective-permute-done.north_ref
  25.9 0.0 copy-start.2
  26.0 0.6 broadcast_in_dim.62
  26.5 0.6 broadcast_in_dim.64
  27.2 0.5 concatenate.7
  27.7 1.9 %collective-permute-start.3 = (bf16[160,128]{1,0:T(8,128)(2,1)S(1)}, bf16[160,128]{1,0:T(8,128)(2,1)S(1)}, u32[]{:S(2)}, u32[]{:S(2)}) collective-permute-start(bf16[160,128]{1,0:T(8,128)(2,1)S(1)} %concatenate.7), channel_id=1, source_target_pairs={{1,0},{2,1},{3,2},{4,3},{5,4},{6,5},{7,6},{8,7},{9,8},{10,9},{11,1... | collective-permute-start | bytes 122888 | tf_op jit(solution)/shard_map/ppermute | solution.py:361
  29.6 0.7 broadcast_in_dim.58
  30.3 0.7 broadcast_in_dim.60
  31.0 0.5 concatenate.6
  31.4 2.4 %collective-permute-start.2 = (bf16[160,128]{1,0:T(8,128)(2,1)S(1)}, bf16[160,128]{1,0:T(8,128)(2,1)S(1)}, u32[]{:S(2)}, u32[]{:S(2)}) collective-permute-start(bf16[160,128]{1,0:T(8,128)(2,1)S(1)} %concatenate.6), channel_id=1, source_target_pairs={{0,1},{1,2},{2,3},{3,4},{4,5},{5,6},{6,7},{7,8},{8,9},{9,10},{10,1... | collective-permute-start | bytes 122888 | tf_op jit(solution)/shard_map/ppermute | solution.py:361
  33.8 1.2 compare_select_fusion.6.dst_ref
  35.0 0.0 collective-permute-done.3.east_ref
  35.0 1.7 %collective-permute-done.2.west_ref = bf16[160,128]{1,0:T(8,128)(2,1)S(1)} collective-permute-done((bf16[160,128]{1,0:T(8,128)(2,1)S(1)}, bf16[160,128]{1,0:T(8,128)(2,1)S(1)}, u32[]{:S(2)}, u32[]{:S(2)}) %collective-permute-start.2) | collective-permute-done | bytes 40992 | tf_op jit(solution)/shard_map/ppermute | solution.py:361
  36.7 0.0 copy-done.3
  36.8 0.0 copy-done.4
  36.8 0.0 copy-done.1
  36.8 0.6 copy-done.6
  37.3 28.8 %both_convs.1 = (bf16[16,32,32,128]{3,2,1,0:T(8,128)(2,1)}, bf16[8,32,32,128]{3,2,1,0:T(8,128)(2,1)}) custom-call(s32[16]{0:T(128)} %reshape.26.wet_ref, s32[4]{0:T(128)} %reshape.27.flag_ref, s32[16]{0:T(128)} %compare_select_fusion.6.dst_ref, bf16[2,8,32,32,128]{4,3,2,1,0:T(8,128)(2,1)} %fields_ref.3, bf16[528,128]{1,0:T(8,128)(2,1)} %copy-done.2, ...), custom_call_target="tpu_custom_call" | custom-call | tf_op jit(solution)/shard_map/both_convs/pallas_call | solution.py:441
  66.1 1.5 %collective-permute-start.4 = (bf16[8,32,32,128]{3,2,1,0:T(8,128)(2,1)}, bf16[8,32,32,128]{3,2,1,0:T(8,128)(2,1)S(1)}, u32[]{:S(2)}, u32[]{:S(2)}) collective-permute-start(bf16[8,32,32,128]{3,2,1,0:T(8,128)(2,1)} %get-tuple-element.15), channel_id=1, source_target_pairs={{0,1},{1,0},{2,3},{3,2},{4,5},{5,4},{6,7},{7,6},{8,9},{9,8},{10,11... | collective-permute-start | bytes 6291464 | tf_op jit(solution)/shard_map/ppermute | solution.py:475
  68.3 1.8 %compare_select_fusion.7.dst_ref = s32[8]{0:T(128)} fusion(s32[]{:T(128)} %get-tuple-element.21, s32[]{:T(128)} %get-tuple-element.20, s32[]{:T(128)S(6)} %select_n.76), kind=kLoop, calls=%fused_computation.19 | loop fusion | flops 248 | bytes 44 | tf_op jit(solution)/shard_map/jit(_where)/select_n | solution.py:411
  70.1 1.5 %collective-permute-done.4.src_ref = bf16[8,32,32,128]{3,2,1,0:T(8,128)(2,1)S(1)} collective-permute-done((bf16[8,32,32,128]{3,2,1,0:T(8,128)(2,1)}, bf16[8,32,32,128]{3,2,1,0:T(8,128)(2,1)S(1)}, u32[]{:S(2)}, u32[]{:S(2)}) %collective-permute-start.4) | collective-permute-done | bytes 2097184 | tf_op jit(solution)/shard_map/ppermute | solution.py:475
  71.7 1.3 copy-done
  73.0 2.7 %merge_mate.1 = bf16[16,32,32,128]{3,2,1,0:T(8,128)(2,1)} custom-call(s32[8]{0:T(128)} %compare_select_fusion.7.dst_ref, bf16[8,32,32,128]{3,2,1,0:T(8,128)(2,1)} %copy-done, bf16[16,32,32,128]{3,2,1,0:T(8,128)(2,1)} %get-tuple-element.16.held_ref), custom_call_target="tpu_custom_call", output_to_operand_aliasing={{}: (2, {})} | custom-call | tf_op jit(solution)/shard_map/merge_mate/pallas_call | solution.py:476
  75.7 0.0 copy-start.9
  75.7 8.8 %all-to-all-start.1 = ((bf16[16,32,32,128]{3,2,1,0:T(8,128)(2,1)}), bf16[16,32,32,128]{3,2,1,0:T(8,128)(2,1)}, u32[]{:S(2)}, u32[]{:S(2)}) async-start(bf16[16,32,32,128]{3,2,1,0:T(8,128)(2,1)} %merge_mate.1), calls=%async_computation.1 | async-start | bytes 8388608 | tf_op jit(solution)/shard_map/all_to_all | solution.py:490
  84.6 0.6 and_select_fusion.6.idx_ref
  85.2 65.7 %all-to-all-done.1.src_ref = bf16[16,32,32,128]{3,2,1,0:T(8,128)(2,1)} async-done(((bf16[16,32,32,128]{3,2,1,0:T(8,128)(2,1)}), bf16[16,32,32,128]{3,2,1,0:T(8,128)(2,1)}, u32[]{:S(2)}, u32[]{:S(2)}) %all-to-all-start.1) | async-done | bytes 4194336 | tf_op jit(solution)/shard_map/all_to_all | solution.py:490
  150.9 3.1 %slot_order.1 = bf16[8,32,32,128]{3,2,1,0:T(8,128)(2,1)} custom-call(s32[8]{0:T(128)} %and_select_fusion.6.idx_ref, bf16[16,32,32,128]{3,2,1,0:T(8,128)(2,1)} %all-to-all-done.1.src_ref), custom_call_target="tpu_custom_call" | custom-call | tf_op jit(solution)/shard_map/slot_order/pallas_call | solution.py:493
  (18 shorter events, 0.1 us)
Async XLA Ops:
  0.0 11.6 %copy-start.8 = (s32[2,8]{1,0:T(2,128)S(1)}, s32[2,8]{1,0:T(2,128)}, u32[]{:S(2)}) copy-start(s32[2,8]{1,0:T(2,128)} %param.10) | copy-start | bytes 196
  3.0 17.8 %copy-start.7 = (s32[16]{0:T(128)S(1)}, s32[16]{0:T(128)}, u32[]{:S(2)}) copy-start(s32[16]{0:T(128)} %reshape.26.wet_ref) | copy-start | bytes 196
  5.7 20.2 %collective-permute-start.1 = (bf16[528,128]{1,0:T(8,128)(2,1)}, bf16[528,128]{1,0:T(8,128)(2,1)S(1)}, u32[]{:S(2)}, u32[]{:S(2)}) collective-permute-start(bf16[528,128]{1,0:T(8,128)(2,1)} %get-tuple-element.12), channel_id=1, source_target_pairs={{32,0},{64,32},{96,64},{33,1},{65,33},{97,65},{34,2},{66,34},{98,6... | collective-permute-start | bytes 405512 | tf_op jit(solution)/shard_map/ppermute | solution.py:361
  7.7 18.2 %collective-permute-start = (bf16[528,128]{1,0:T(8,128)(2,1)}, bf16[528,128]{1,0:T(8,128)(2,1)S(1)}, u32[]{:S(2)}, u32[]{:S(2)}) collective-permute-start(bf16[528,128]{1,0:T(8,128)(2,1)} %get-tuple-element.11), channel_id=1, source_target_pairs={{0,32},{32,64},{64,96},{1,33},{33,65},{65,97},{2,34},{34,66},{66,9... | collective-permute-start | bytes 405512 | tf_op jit(solution)/shard_map/ppermute | solution.py:361
  13.5 11.1 %all-to-all-start = ((s32[32,1,1]{2,1,0:T(1,128)}), s32[32,1,1]{2,1,0:T(1,128)S(1)}, u32[]{:S(2)}, u32[]{:S(2)}) async-start(s32[32,1,1]{2,1,0:T(1,128)} %broadcast_in_dim.53), calls=%async_computation | async-start | bytes 32768 | tf_op jit(solution)/shard_map/all_to_all | solution.py:398
  21.6 15.1 %copy-start.3 = (bf16[64,128]{1,0:T(8,128)(2,1)}, bf16[64,128]{1,0:T(8,128)(2,1)S(1)}, u32[]{:S(2)}) copy-start(bf16[64,128]{1,0:T(8,128)(2,1)S(1)} %get-tuple-element.47.lcol_ref) | copy-start | bytes 49156
  22.4 14.4 %copy-start.4 = (bf16[64,128]{1,0:T(8,128)(2,1)}, bf16[64,128]{1,0:T(8,128)(2,1)S(1)}, u32[]{:S(2)}) copy-start(bf16[64,128]{1,0:T(8,128)(2,1)S(1)} %get-tuple-element.48.rcol_ref) | copy-start | bytes 49156
  25.9 10.9 %copy-start.1 = (bf16[528,128]{1,0:T(8,128)(2,1)}, bf16[528,128]{1,0:T(8,128)(2,1)S(1)}, u32[]{:S(2)}) copy-start(bf16[528,128]{1,0:T(8,128)(2,1)S(1)} %collective-permute-done.1.south_ref) | copy-start | bytes 405508
  25.9 10.8 %copy-start.2 = (bf16[528,128]{1,0:T(8,128)(2,1)}, bf16[528,128]{1,0:T(8,128)(2,1)S(1)}, u32[]{:S(2)}) copy-start(bf16[528,128]{1,0:T(8,128)(2,1)S(1)} %collective-permute-done.north_ref) | copy-start | bytes 405508
  27.7 7.4 %collective-permute-start.3 = (bf16[160,128]{1,0:T(8,128)(2,1)S(1)}, bf16[160,128]{1,0:T(8,128)(2,1)S(1)}, u32[]{:S(2)}, u32[]{:S(2)}) collective-permute-start(bf16[160,128]{1,0:T(8,128)(2,1)S(1)} %concatenate.7), channel_id=1, source_target_pairs={{1,0},{2,1},{3,2},{4,3},{5,4},{6,5},{7,6},{8,7},{9,8},{10,9},{11,1... | collective-permute-start | bytes 122888 | tf_op jit(solution)/shard_map/ppermute | solution.py:361
  31.4 5.3 %collective-permute-start.2 = (bf16[160,128]{1,0:T(8,128)(2,1)S(1)}, bf16[160,128]{1,0:T(8,128)(2,1)S(1)}, u32[]{:S(2)}, u32[]{:S(2)}) collective-permute-start(bf16[160,128]{1,0:T(8,128)(2,1)S(1)} %concatenate.6), channel_id=1, source_target_pairs={{0,1},{1,2},{2,3},{3,4},{4,5},{5,6},{6,7},{7,8},{8,9},{9,10},{10,1... | collective-permute-start | bytes 122888 | tf_op jit(solution)/shard_map/ppermute | solution.py:361
  35.0 1.8 %copy-start.5 = (bf16[160,128]{1,0:T(8,128)(2,1)}, bf16[160,128]{1,0:T(8,128)(2,1)S(1)}, u32[]{:S(2)}) copy-start(bf16[160,128]{1,0:T(8,128)(2,1)S(1)} %collective-permute-done.3.east_ref) | copy-start | bytes 122884
  36.7 0.6 copy-start.6
  66.1 5.5 %collective-permute-start.4 = (bf16[8,32,32,128]{3,2,1,0:T(8,128)(2,1)}, bf16[8,32,32,128]{3,2,1,0:T(8,128)(2,1)S(1)}, u32[]{:S(2)}, u32[]{:S(2)}) collective-permute-start(bf16[8,32,32,128]{3,2,1,0:T(8,128)(2,1)} %get-tuple-element.15), channel_id=1, source_target_pairs={{0,1},{1,0},{2,3},{3,2},{4,5},{5,4},{6,7},{7,6},{8,9},{9,8},{10,11... | collective-permute-start | bytes 6291464 | tf_op jit(solution)/shard_map/ppermute | solution.py:475
  71.7 1.3 copy-start
  75.7 8.8 %copy-start.9 = (s32[8]{0:T(128)S(1)}, s32[8]{0:T(128)}, u32[]{:S(2)}) copy-start(s32[8]{0:T(128)} %param.12) | copy-start | bytes 100
  75.7 75.2 %all-to-all-start.1 = ((bf16[16,32,32,128]{3,2,1,0:T(8,128)(2,1)}), bf16[16,32,32,128]{3,2,1,0:T(8,128)(2,1)}, u32[]{:S(2)}, u32[]{:S(2)}) async-start(bf16[16,32,32,128]{3,2,1,0:T(8,128)(2,1)} %merge_mate.1), calls=%async_computation.1 | async-start | bytes 8388608 | tf_op jit(solution)/shard_map/all_to_all | solution.py:490

commit v2 on v1

--- a/solution.py
+++ b/solution.py
@@ -9,10 +9,11 @@
 
 F32 = jnp.float32
 BF16 = jnp.bfloat16
-VMEM_LIMIT = 56 * 1024 * 1024
+VMEM_LIMIT = 32 * 1024 * 1024
 WHOLE = pl.BlockSpec(memory_space=pltpu.VMEM)
 SCALARS = pl.BlockSpec(memory_space=pltpu.SMEM)
 IN_PLACE = pl.BlockSpec(memory_space=pl.ANY)
+IN_HBM = pl.BlockSpec(memory_space=pltpu.HBM)
 
 
 def dot(a, b):
@@ -65,7 +66,7 @@
         t_ref[at : at + 1] = ext_ref[from_row : from_row + 1]
         middle = ext_ref[from_row + 1 : from_row + 1 + tile]
         turned = dot(flip, middle.astype(BF16))
-        t_ref[at + 1 : at + 1 + tile] = jnp.where(flag == 1, turned, middle)
+        t_ref[at + 1 : at + 1 + tile] = jnp.where(flag > 0.5, turned, middle)
         t_ref[at + tall - 1 : at + tall] = ext_ref[from_row + tile + 1 : from_row + tile + 2]
     last = 3 + tall * len(flags)
     for n, line in enumerate(below):
@@ -100,8 +101,12 @@
     return outs
 
 
+def seam_line(seam_ref, i, j, side, ch):
+    return jnp.full((1, ch), 1.0, F32) * seam_ref[i, side, j].astype(F32)
+
+
 def rim_kernel(
-    wet_ref, flag_ref, fields_ref, top_ref, bottom_ref, lcol_ref, rcol_ref,
+    wet_ref, seam_ref, fields_ref, top_ref, bottom_ref, lcol_ref, rcol_ref, count_ref,
     rows_ref, cols_ref, line_ref, sems,
 ):
     tr_dev, tc_dev, tile, _, ch = fields_ref.shape
@@ -115,12 +120,14 @@
     ]
     for load in loads:
         load.start()
+
+    def wet(i, j):
+        return jnp.full((1, ch), 1.0, F32) * wet_ref[i, j].astype(F32)
+
+    total = sum(wet_ref[i, j] for i in range(tr_dev) for j in range(tc_dev))
+    count_ref[...] = jnp.full(count_ref.shape, 1.0, F32) * total.astype(F32)
     for load in loads:
         load.wait()
-
-    def wet(i, j):
-        return jnp.full((1, ch), 1.0, F32) * wet_ref[i * tc_dev + j].astype(F32)
-
     for side, (out_ref, i) in enumerate(((top_ref, 0), (bottom_ref, tr_dev - 1))):
         for j in range(tc_dev):
             scale = wet(i, j).astype(BF16)
@@ -139,9 +146,11 @@
         out_ref[1] = columns[1].astype(BF16)
         picked.append(columns[side])
     for out_ref, i, near in ((top_ref, 0, tile - 2), (bottom_ref, tr_dev - 1, tile * (tr_dev - 1))):
-        flags = [jnp.full((1, ch), 1.0, F32) * flag_ref[2 * i + side].astype(F32) for side in range(2)]
         extra = [column[near : near + 2] for column in picked]
-        extra += [wet(i, j) for j in range(tc_dev)] + flags
+        extra += [wet(i, j) for j in range(tc_dev)]
+        extra += [
+            seam_line(seam_ref, i, side * (tc_dev - 1), side, ch) for side in range(2)
+        ]
         extra.append(jnp.zeros((12 - tc_dev - 2, ch), F32))
         at = 0
         for piece in extra:
@@ -150,10 +159,50 @@
         out_ref[2 * width : 2 * width + 16] = line_ref[0, 0:16].astype(BF16)
 
 
+def pixel(ref, n):
+    base = n // 16 * 16
+    return ref[base : base + 16].astype(F32)[n - base : n - base + 1]
+
+
+def side_kernel(wet_ref, north_ref, south_ref, lcol_ref, rcol_ref, left_ref, right_ref, line_ref):
+    tr_dev, tc_dev = wet_ref.shape
+    ch = north_ref.shape[1]
+    height = lcol_ref.shape[1]
+    width = (north_ref.shape[0] - 16) // 2
+    span = height + 8
+    notes = [ref[2 * width : 2 * width + 16].astype(F32) for ref in (north_ref, south_ref)]
+    for s, (out_ref, own) in enumerate(((left_ref, lcol_ref), (right_ref, rcol_ref))):
+        for n in range(2):
+            c = s * (width - 2) + n
+            at = n * span
+            line_ref[at : at + 1] = pixel(north_ref, c)
+            line_ref[at + 1 : at + 2] = pixel(north_ref, width + c)
+            line_ref[at + 2 : at + 2 + height] = own[n].astype(F32)
+            line_ref[at + 2 + height : at + 3 + height] = pixel(south_ref, c)
+            line_ref[at + 3 + height : at + 4 + height] = pixel(south_ref, width + c)
+            line_ref[at + 4 + height : at + span] = jnp.zeros((4, ch), F32)
+        at = 2 * span
+        j = s * (tc_dev - 1)
+        line_ref[at : at + 16] = jnp.zeros((16, ch), F32)
+        line_ref[at : at + 2] = notes[0][2 * s : 2 * s + 2]
+        line_ref[at + 2 : at + 4] = notes[1][2 * s : 2 * s + 2]
+        for i in range(tr_dev):
+            line_ref[at + 4 + i : at + 5 + i] = jnp.full((1, ch), 1.0, F32) * wet_ref[i, j].astype(F32)
+        line_ref[at + 4 + tr_dev : at + 5 + tr_dev] = notes[0][4 + j : 5 + j]
+        line_ref[at + 5 + tr_dev : at + 6 + tr_dev] = notes[1][4 + j : 5 + j]
+        out_ref[...] = line_ref[...].astype(BF16)
+
+
+def wet_before(count_ref, place):
+    row = lax.broadcasted_iota(jnp.int32, count_ref.shape, 0)
+    earlier = jnp.where(row < place, count_ref[...], 0.0)
+    return jnp.max(jnp.sum(earlier, axis=0)).astype(jnp.int32)
+
+
 def conv_kernel(
-    wet_ref, flag_ref, dst_ref, fields_ref, north_ref, south_ref, west_ref, east_ref,
+    wet_ref, seam_ref, count_ref, fields_ref, north_ref, south_ref, west_ref, east_ref,
     lcol_ref, rcol_ref, k1_ref, b1_ref, k2_ref, b2_ref, mix_ref, keep_ref, give_ref,
-    out_ref, x_ref, hid_ref, w1_ref, w2_ref, mm_ref, m_ref, pack_ref, own_ref, ext_ref, t_ref,
+    own_tiles, out_ref, x_ref, hid_ref, br_ref, w1_ref, w2_ref, mm_ref, m_ref, pack_ref, own_ref, ext_ref, t_ref,
     zw1_ref, ze1_ref, zw2_ref, ze2_ref, in_sems, sems,
 ):
     tr_dev, tc_dev, tile, _, ch = fields_ref.shape
@@ -162,7 +211,7 @@
     tall = 3 + (tile + 2) * tr_dev + 3
     lines = tall - 2
     loads = [
-        pltpu.make_async_copy(fields_ref.at[i], out_ref.at[i], in_sems.at[i]) for i in range(tr_dev)
+        pltpu.make_async_copy(fields_ref.at[i], own_tiles.at[i], in_sems.at[i]) for i in range(tr_dev)
     ]
     for load in loads:
         load.start()
@@ -182,12 +231,8 @@
     notes = [ref[2 * width : 2 * width + 16].astype(F32) for ref in (north_ref, south_ref)]
     flagged = [[note[4 + tc_dev + s : 5 + tc_dev + s] > 0.5 for s in range(2)] for note in notes]
 
-    def pixel(ref, n):
-        base = n // 16 * 16
-        return ref[base : base + 16].astype(F32)[n - base : n - base + 1]
-
-    step_size = pack_ref.shape[1] // 20 * 9
-    sides = ((west_ref, lcol_ref, 0), (east_ref, rcol_ref, width - 1))
+    step_size = height + 8
+    sides = ((west_ref, lcol_ref.at[0], 0), (east_ref, rcol_ref.at[1], width - 1))
     for s, (pack, own, c) in enumerate(sides):
         pack_ref[s] = pack[...].astype(F32)
         own_ref[s, 1 : height + 1] = own[...].astype(F32)
@@ -200,7 +245,7 @@
         note = [pack_ref[s, notes_at + n : notes_at + n + 1] for n in range(8)]
         held = pack_ref.at[s]
         mine = own_ref.at[s]
-        flags = [flag_ref[2 * i + s] for i in range(tr_dev)]
+        flags = [seam_line(seam_ref, i, s * (tc_dev - 1), s, ch) for i in range(tr_dev)]
         north_flag, south_flag = flagged[0][s], flagged[1][s]
 
         def near_line(n, near=near, held=held):
@@ -249,20 +294,23 @@
 
     x_ref[0] = north_ref[width : 2 * width]
     x_ref[height + 1] = south_ref[0:width]
-    for i in range(tr_dev):
+
+    def fill(i):
         loads[i].wait()
         for j in range(tc_dev):
-            scale = jnp.full((1, ch), 1.0, F32) * wet_ref[i * tc_dev + j].astype(F32)
+            scale = jnp.full((1, ch), 1.0, F32) * wet_ref[i, j].astype(F32)
             m_ref[i, j * tile : (j + 1) * tile] = jnp.broadcast_to(scale, (tile, ch))
             x_ref[1 + i * tile : 1 + (i + 1) * tile, j * tile : (j + 1) * tile] = (
-                out_ref[i, j] * scale.astype(BF16)[None]
+                own_tiles[i, j] * scale.astype(BF16)[None]
             )
 
     beyond = (
-        (0, [north_ref[0:width], north_ref[width : 2 * width], x_ref[1]], 0, notes[0]),
-        (height + 1, [x_ref[height], south_ref[0:width], south_ref[width : 2 * width]], lines - 1, notes[1]),
+        (0, [north_ref.at[0:width], north_ref.at[width : 2 * width], x_ref.at[1]], 0, notes[0]),
+        (height + 1, [x_ref.at[height], south_ref.at[0:width], south_ref.at[width : 2 * width]], lines - 1, notes[1]),
     )
-    for row, window, line, note in beyond:
+
+    def outside(row, window, line, note):
+        window = [w[...] for w in window]
         z = dot(jnp.concatenate(window, axis=1), w1_ref[: 3 * ch, : 3 * ch])
         total = side_sums(z, 0, zw1_ref[line : line + 1], ze1_ref[line : line + 1]) + bias1
         value = gelu(total)
@@ -279,105 +327,124 @@
             hid_ref[1 + row + ro] = (gelu(outs[ro]) * m_ref[row // tile]).astype(BF16)
         return carry
 
-    def second(p, carry):
+    def branch(p):
         row = 2 * p
-        i = row // tile
-        inner = row % tile
         window = [hid_ref[row + k] for k in range(4)]
         outs = conv_pair(window, w2_ref, bias2, zw2_ref, ze2_ref, line_at(row, tile))
-        branch = jnp.concatenate([gelu(o).astype(BF16) for o in outs], axis=1)
-        mixed = dot(branch, mm_ref[...])
         for ro in range(2):
-            own = out_ref[i, :, inner + ro].reshape(width, ch).astype(F32)
+            br_ref[p, :, ro * ch : (ro + 1) * ch] = gelu(outs[ro]).astype(BF16)
+
+    def mix(p):
+        i = 2 * p // tile
+        inner = 2 * p % tile
+        mixed = dot(br_ref[p], mm_ref[...])
+        for ro in range(2):
+            own = own_tiles[i, :, inner + ro].reshape(width, ch).astype(F32)
             total = (own + mixed[:, ro * ch : (ro + 1) * ch]).astype(BF16)
             out_ref[i, :, inner + ro] = total.reshape(tc_dev, tile, ch)
+
+    def second(p, carry):
+        branch(p)
         return carry
 
-    def copies(i, act):
+    def third(p, carry):
+        mix(p)
+        return carry
+
+    place = lax.axis_index("col")
+    rank = wet_before(count_ref, place)
+    odd = place % 2
+    targets = []
+    given = 0
+    for i in range(tr_dev):
+        for j in range(tc_dev):
+            kept = rank % 2 == odd
+            slot = jnp.where(kept, rank % (2 * slots) // 2, slots + given // 2)
+            targets.append(jnp.where(wet_ref[i, j] == 1, slot, -1))
+            rank += wet_ref[i, j]
+            given += wet_ref[i, j]
+
+    def start_copies(i):
         for j in range(tc_dev):
             k = i * tc_dev + j
-            target = dst_ref[k]
+            target = targets[k]
 
             @pl.when((target >= 0) & (target < slots))
             def _():
-                act(pltpu.make_async_copy(out_ref.at[i, j], keep_ref.at[target], sems.at[k]))
+                pltpu.make_async_copy(out_ref.at[i, j], keep_ref.at[target], sems.at[k]).start()
 
             @pl.when(target >= slots)
             def _():
-                act(pltpu.make_async_copy(out_ref.at[i, j], give_ref.at[target - slots], sems.at[k]))
-
-    lax.fori_loop(0, height // 2, first, 0, unroll=4)
+                pltpu.make_async_copy(
+                    out_ref.at[i, j], give_ref.at[target - slots], sems.at[k]
+                ).start()
+
+    def wait_copies(i):
+        for j in range(tc_dev):
+            k = i * tc_dev + j
+
+            @pl.when(wet_ref[i, j] == 1)
+            def _():
+                pltpu.make_async_copy(out_ref.at[i, j], keep_ref.at[0], sems.at[k]).wait()
+
+    done = 0
     for i in range(tr_dev):
-        lax.fori_loop(i * tile // 2, (i + 1) * tile // 2, second, 0, unroll=4)
-        copies(i, lambda c: c.start())
+        fill(i)
+        if i == 0:
+            outside(*beyond[0])
+        if i == tr_dev - 1:
+            outside(*beyond[1])
+        ready = (i + 1) * tile // 2 - (i < tr_dev - 1)
+        lax.fori_loop(done, ready, first, 0, unroll=ready - done)
+        done = ready
     for i in range(tr_dev):
-        copies(i, lambda c: c.wait())
-
-
-def scatter_kernel(dst_ref, src_ref, held_ref, out_ref, buf_ref, in_sems, sems):
+        lax.fori_loop(i * tile // 2, (i + 1) * tile // 2, second, 0, unroll=tile // 2)
+        lax.fori_loop(i * tile // 2, (i + 1) * tile // 2, third, 0, unroll=8)
+        start_copies(i)
+    for i in range(tr_dev):
+        wait_copies(i)
+
+
+def scatter_kernel(count_ref, src_ref, held_ref, out_ref, sems):
+    slots = out_ref.shape[0]
+    place = lax.axis_index("col")
+    odd = place % 2
+    mate = place + 1 - 2 * odd
+    start = wet_before(count_ref, mate)
+    stop = wet_before(count_ref, mate + 1)
+    ranks = [start + 2 * k + (start + odd) % 2 for k in range(src_ref.shape[0])]
+
     def each(act):
-        for k in range(src_ref.shape[0]):
-
-            @pl.when(dst_ref[k] >= 0)
+        for k, rank in enumerate(ranks):
+
+            @pl.when(rank < stop)
             def _():
                 act(k)
 
-    def load(k):
-        return pltpu.make_async_copy(src_ref.at[k], buf_ref.at[k], in_sems.at[k])
-
     def store(k):
-        return pltpu.make_async_copy(buf_ref.at[k], out_ref.at[dst_ref[k]], sems.at[k])
-
-    def turn(k):
-        load(k).wait()
-        store(k).start()
-
-    each(lambda k: load(k).start())
-    each(turn)
+        slot = ranks[k] % (2 * slots) // 2
+        return pltpu.make_async_copy(src_ref.at[k], out_ref.at[slot], sems.at[k])
+
+    each(lambda k: store(k).start())
     each(lambda k: store(k).wait())
 
 
-def gather_kernel(idx_ref, src_ref, out_ref, buf_ref, in_sems, sems):
-    count = out_ref.shape[0]
-
-    def load(k):
-        return pltpu.make_async_copy(src_ref.at[idx_ref[k]], buf_ref.at[k], in_sems.at[k])
-
-    def store(k):
-        return pltpu.make_async_copy(buf_ref.at[k], out_ref.at[k], sems.at[k])
-
-    for k in range(count):
-        load(k).start()
-    for k in range(count):
-        load(k).wait()
-        store(k).start()
-    for k in range(count):
-        store(k).wait()
+def gather_kernel(across, list_ref, src_ref, out_ref, sems):
+    chips = src_ref.shape[0]
+    copies = []
+    for k in range(out_ref.shape[0]):
+        chip = list_ref[k] % across // (across // chips)
+        copies.append(pltpu.make_async_copy(src_ref.at[chip], out_ref.at[k], sems.at[k]))
+    for copy in copies:
+        copy.start()
+    for copy in copies:
+        copy.wait()
 
 
 def shifted(x, axis, step):
     count = lax.axis_size(axis)
     pairs = [(i, i + step) for i in range(count) if 0 <= i + step < count]
     return lax.ppermute(x, axis, pairs)
-
-
-def side_pack(north, south, columns, at, wets):
-    width = (north.shape[0] - 16) // 2
-    tc_dev = 8
-    filler = jnp.zeros((4, north.shape[1]), north.dtype)
-    pieces = []
-    for n in range(2):
-        c = at + n
-        pieces += [north[c : c + 1], north[width + c : width + c + 1], columns[n]]
-        pieces += [south[c : c + 1], south[width + c : width + c + 1], filler]
-    side = 1 if at else 0
-    tile = at and tc_dev - 1
-    base = 2 * width
-    pieces += [ref[base + 2 * side : base + 2 * side + 2] for ref in (north, south)]
-    pieces += wets
-    pieces += [ref[base + 4 + tile : base + 5 + tile] for ref in (north, south)]
-    pieces.append(jnp.zeros((8, north.shape[1]), north.dtype))
-    return jnp.concatenate(pieces, axis=0)
 
 
 def on_device(
@@ -389,51 +456,43 @@
     columns = lax.axis_size("col")
     chips = columns // 2
     width, height = tc_dev * tile, tr_dev * tile
-    me = lax.axis_index("col")
-    core = me % 2
-    wet = wet_mask.reshape(face)
-    flags = jnp.stack([seam_flags[:, 0, 0], seam_flags[:, tc_dev - 1, 1]], axis=1).reshape(-1)
-
-    total = jnp.broadcast_to(jnp.sum(wet), (columns, 1, 1))
-    counts = lax.all_to_all(total, "col", split_axis=0, concat_axis=0, tiled=True).reshape(columns)
-    cids = jnp.arange(columns)
-    start = jnp.sum(jnp.where(cids < me, counts, 0))
-    mate = me ^ 1
-    mate_start = jnp.sum(jnp.where(cids < mate, counts, 0))
-    mate_count = jnp.sum(jnp.where(cids == mate, counts, 0))
-    ids = jnp.arange(face)
-    local = jnp.sum(jnp.where(ids[None, :] < ids[:, None], wet[None, :], 0), axis=1)
-    rank = start + local
-    slot = (rank % columns) // 2
-    dst = jnp.where(wet == 1, jnp.where(rank % 2 == core, slot, chips + local // 2), -1)
     half = face // 2
-    mate_local = 2 * jnp.arange(half) + (mate_start + core) % 2
-    mate_dst = jnp.where(mate_local < mate_count, ((mate_start + mate_local) % columns) // 2, -1)
-    source_chip = (wet_list % (tc_dev * columns)) // (2 * tc_dev)
-
+    seams = jnp.swapaxes(seam_flags, 1, 2)
     params = pltpu.CompilerParams(vmem_limit_bytes=VMEM_LIMIT)
+    small = pltpu.CompilerParams(vmem_limit_bytes=VMEM_LIMIT // 8)
+    fields = pltpu.with_memory_space_constraint(fields, pltpu.HBM)
     strip = jax.ShapeDtypeStruct((2 * width + 16, ch), BF16)
     pair = jax.ShapeDtypeStruct((2, height, ch), BF16)
-    top, bottom, lcols, rcols = pl.pallas_call(
+    top, bottom, lcols, rcols, count = pl.pallas_call(
         rim_kernel,
-        out_shape=(strip, strip, pair, pair),
-        in_specs=[SCALARS, SCALARS, IN_PLACE],
-        out_specs=(WHOLE,) * 4,
+        out_shape=(strip, strip, pair, pair, jax.ShapeDtypeStruct((columns, 1, ch), F32)),
+        in_specs=[SCALARS, SCALARS, IN_HBM],
+        out_specs=(WHOLE,) * 5,
         scratch_shapes=[
             pltpu.VMEM((2, tc_dev, 2, tile, ch), BF16),
             pltpu.VMEM((2, tr_dev, tile, 16, ch), BF16),
             pltpu.VMEM((2, height * 16, ch), F32),
             pltpu.SemaphoreType.DMA((4,)),
         ],
+        compiler_params=small,
         name="rim",
-    )(wet, flags, fields)
+    )(wet_mask, seams, fields)
     north = shifted(bottom, "row", 1)
     south = shifted(top, "row", -1)
-    wets = jnp.broadcast_to(wet_mask.astype(BF16)[:, :, None, None], (tr_dev, tc_dev, 1, ch))
-    west = shifted(
-        side_pack(north, south, rcols, width - 2, [wets[i, -1] for i in range(tr_dev)]), "col", 1
-    )
-    east = shifted(side_pack(north, south, lcols, 0, [wets[i, 0] for i in range(tr_dev)]), "col", -1)
+    counts = lax.all_to_all(count, "col", split_axis=0, concat_axis=0, tiled=True)
+    pack = jax.ShapeDtypeStruct((2 * (height + 8) + 16, ch), BF16)
+    left, right = pl.pallas_call(
+        side_kernel,
+        out_shape=(pack, pack),
+        in_specs=[SCALARS] + [WHOLE] * 4,
+        out_specs=(WHOLE,) * 2,
+        scratch_shapes=[pltpu.VMEM(pack.shape, F32)],
+        compiler_params=small,
+        name="side",
+    )(wet_mask, north, south, lcols, rcols)
+    left, right, counts = lax.optimization_barrier((left, right, counts))
+    west = shifted(right, "col", 1)
+    east = shifted(left, "col", -1)
 
     tile_shape = (tile, tile, ch)
     lines = 8 + (tile + 2) * tr_dev
@@ -444,12 +503,14 @@
             jax.ShapeDtypeStruct((chips,) + tile_shape, BF16),
             jax.ShapeDtypeStruct((half,) + tile_shape, BF16),
         ),
-        in_specs=[SCALARS] * 3 + [IN_PLACE] + [WHOLE] * 11,
+        in_specs=[SCALARS, SCALARS, WHOLE, IN_HBM] + [WHOLE] * 11,
         out_specs=(IN_PLACE, IN_PLACE),
         scratch_shapes=[
             pltpu.VMEM(fields.shape, BF16),
+            pltpu.VMEM(fields.shape, BF16),
             pltpu.VMEM((height + 2, width, ch), BF16),
             pltpu.VMEM((height + 2, width, ch), BF16),
+            pltpu.VMEM((height // 2, width, 2 * ch), BF16),
             pltpu.VMEM((4 * ch, 6 * ch), BF16),
             pltpu.VMEM((4 * ch, 6 * ch), BF16),
             pltpu.VMEM((2 * ch, 2 * ch), BF16),
@@ -468,7 +529,7 @@
         compiler_params=params,
         name="both_convs",
     )(
-        wet, flags, dst, fields, north, south, west, east, lcols[0], rcols[1],
+        wet_mask, seams, counts, fields, north, south, west, east, lcols, rcols,
         kernel_one, bias_one[None], kernel_two, bias_two[None], mixing,
     )
 
@@ -476,32 +537,26 @@
     sending = pl.pallas_call(
         scatter_kernel,
         out_shape=jax.ShapeDtypeStruct(keep.shape, BF16),
-        in_specs=[SCALARS, IN_PLACE, IN_PLACE],
+        in_specs=[WHOLE, WHOLE, IN_PLACE],
         out_specs=IN_PLACE,
-        scratch_shapes=[
-            pltpu.VMEM((half,) + tile_shape, BF16),
-            pltpu.SemaphoreType.DMA((half,)),
-            pltpu.SemaphoreType.DMA((half,)),
-        ],
+        scratch_shapes=[pltpu.SemaphoreType.DMA((half,))],
         input_output_aliases={2: 0},
+        compiler_params=small,
         name="merge_mate",
-    )(mate_dst, taken, keep)
+    )(counts, taken, keep)
     groups = [[2 * k + c for k in range(chips)] for c in range(2)]
     arrived = lax.all_to_all(
         sending, "col", split_axis=0, concat_axis=0, tiled=True, axis_index_groups=groups
     )
     return pl.pallas_call(
-        gather_kernel,
+        functools.partial(gather_kernel, tc_dev * columns),
         out_shape=jax.ShapeDtypeStruct((wet_dev,) + tile_shape, BF16),
-        in_specs=[SCALARS, IN_PLACE],
-        out_specs=IN_PLACE,
-        scratch_shapes=[
-            pltpu.VMEM((wet_dev,) + tile_shape, BF16),
-            pltpu.SemaphoreType.DMA((wet_dev,)),
-            pltpu.SemaphoreType.DMA((wet_dev,)),
-        ],
+        in_specs=[SCALARS, WHOLE],
+        out_specs=IN_HBM,
+        scratch_shapes=[pltpu.SemaphoreType.DMA((wet_dev,))],
+        compiler_params=small,
         name="slot_order",
-    )(source_chip, arrived)
+    )(wet_list, arrived)
 
 
 def solution(mesh):

time: 156 us -> 120 us (0.77)
  the two profiles are of different devices: /device:TPU:92 before, /device:TPU:32 now
where the time goes in v2:
time: 120 us
  blocking collectives  58.9 us (49%)
  Pallas kernels  27.4 us (23%)
  starting transfers between devices  18.9 us (16%)
  waiting for transfers between devices  12.6 us (10%)
  local copies, waits for them, and re-layouts  1.45 us (1%)
    all_to_all x1, blocking collectives, on_device(): lax.all_to_all(sending, 'col', split_axis=0, concat_axis=0, tiled=True, a...  58.9 us
    pallas_call x1, Pallas kernels, on_device(): pl.pallas_call(conv_kernel, out_shape=(jax.ShapeDtypeStruct((chips,) + ti...  22 us
    ppermute x4, starting transfers between devices, shifted(): return lax.ppermute(x, axis, pairs)  8.89 us
    all_to_all x1, starting transfers between devices, on_device(): lax.all_to_all(count, 'col', split_axis=0, concat_axis=0, tiled=True)  7.33 us
    all_to_all x1, waiting for transfers between devices, on_device(): lax.all_to_all(count, 'col', split_axis=0, concat_axis=0, tiled=True)  6.67 us
    ppermute x1, waiting for transfers between devices, on_device(): taken = lax.ppermute(give, 'col', [(i, i ^ 1) for i in range(columns)])  3.79 us
    ppermute x1, starting transfers between devices, on_device(): taken = lax.ppermute(give, 'col', [(i, i ^ 1) for i in range(columns)])  2.7 us
    pallas_call x1, Pallas kernels, on_device(): pl.pallas_call(rim_kernel, out_shape=(strip, strip, pair, pair, jax.Shape...  2.43 us
  transfers between devices with their start and end apart: 6, of which 3 were waited for; matrix products, arithmetic and copies ran while one was open for 0% of the time, Pallas kernels for 0%

profile of v2, /device:TPU:32, one launch (start us, length us, event | category | flops | bytes accessed | tf_op | source)
XLA Modules:
  0.0 119.5 jit_solution(6748367311032617350)
XLA Ops:
  0.0 0.0 copy-start.2
  0.0 0.0 copy-start.1
  0.0 0.0 copy-start
  0.0 0.0 copy-start.3
  0.0 0.7 copy-done.3
  0.8 0.0 copy-start.5
  0.8 0.7 copy-done.5
  1.4 0.0 copy-start.4
  1.4 0.0 copy-start.6
  1.4 0.0 copy-start.7
  1.4 0.0 copy-start.8
  1.4 2.4 %rim.1 = (bf16[528,128]{1,0:T(8,128)(2,1)S(1)}, bf16[528,128]{1,0:T(8,128)(2,1)S(1)}, bf16[2,64,128]{2,1,0:T(8,128)(2,1)S(1)}, bf16[2,64,128]{2,1,0:T(8,128)(2,1)S(1)}, f32[32,1,128]{2,1,0:T(1,128)}) custom-call(s32[2,8]{1,0:T(2,128)S(1)} %copy-done.3, s32[2,2,8]{2,1,0:T(2,128)S(1)} %bitcast.3, bf16[2,8,32,32,128]{4,3,2,1,0:T(8,128)(2,1)} %fields_ref.3), custom_call_target="tpu_custom_call" | custom-call | tf_op jit(solution)/shard_map/rim/pallas_call | solution.py:466
  3.9 3.8 %collective-permute-start = (bf16[528,128]{1,0:T(8,128)(2,1)S(1)}, bf16[528,128]{1,0:T(8,128)(2,1)S(1)}, u32[]{:S(2)}, u32[]{:S(2)}) collective-permute-start(bf16[528,128]{1,0:T(8,128)(2,1)S(1)} %get-tuple-element.17), channel_id=1, source_target_pairs={{0,32},{32,64},{64,96},{1,33},{33,65},{65,97},{2,34},{34,66},{66,9... | collective-permute-start | bytes 405512 | tf_op jit(solution)/shard_map/ppermute | solution.py:447
  7.7 2.0 %collective-permute-start.1 = (bf16[528,128]{1,0:T(8,128)(2,1)S(1)}, bf16[528,128]{1,0:T(8,128)(2,1)S(1)}, u32[]{:S(2)}, u32[]{:S(2)}) collective-permute-start(bf16[528,128]{1,0:T(8,128)(2,1)S(1)} %get-tuple-element.18), channel_id=1, source_target_pairs={{32,0},{64,32},{96,64},{33,1},{65,33},{97,65},{34,2},{66,34},{98,6... | collective-permute-start | bytes 405512 | tf_op jit(solution)/shard_map/ppermute | solution.py:447
  9.7 7.3 %all-to-all-start = ((f32[32,1,128]{2,1,0:T(1,128)}), f32[32,1,128]{2,1,0:T(1,128)S(1)}, u32[]{:S(2)}, u32[]{:S(2)}) async-start(f32[32,1,128]{2,1,0:T(1,128)} %get-tuple-element.23), calls=%async_computation | async-start | bytes 32768 | tf_op jit(solution)/shard_map/all_to_all | solution.py:482
  17.1 0.0 collective-permute-done.north_ref
  17.1 0.0 collective-permute-done.1.south_ref
  17.1 0.0 copy-done.4
  17.1 0.6 side.1
  17.7 6.7 %all-to-all-done.count_ref = f32[32,1,128]{2,1,0:T(1,128)S(1)} async-done(((f32[32,1,128]{2,1,0:T(1,128)}), f32[32,1,128]{2,1,0:T(1,128)S(1)}, u32[]{:S(2)}, u32[]{:S(2)}) %all-to-all-start) | async-done | bytes 16416 | tf_op jit(solution)/shard_map/all_to_all | solution.py:482
  24.4 1.7 %collective-permute-start.2 = (bf16[160,128]{1,0:T(8,128)(2,1)S(1)}, bf16[160,128]{1,0:T(8,128)(2,1)S(1)}, u32[]{:S(2)}, u32[]{:S(2)}) collective-permute-start(bf16[160,128]{1,0:T(8,128)(2,1)S(1)} %get-tuple-element.25), channel_id=1, source_target_pairs={{0,1},{1,2},{2,3},{3,4},{4,5},{5,6},{6,7},{7,8},{8,9},{9,10},{10,1... | collective-permute-start | bytes 122888 | tf_op jit(solution)/shard_map/ppermute | solution.py:447
  26.1 1.3 %collective-permute-start.3 = (bf16[160,128]{1,0:T(8,128)(2,1)S(1)}, bf16[160,128]{1,0:T(8,128)(2,1)S(1)}, u32[]{:S(2)}, u32[]{:S(2)}) collective-permute-start(bf16[160,128]{1,0:T(8,128)(2,1)S(1)} %get-tuple-element.26), channel_id=1, source_target_pairs={{1,0},{2,1},{3,2},{4,3},{5,4},{6,5},{7,6},{8,7},{9,8},{10,9},{11,1... | collective-permute-start | bytes 122888 | tf_op jit(solution)/shard_map/ppermute | solution.py:447
  27.4 0.0 collective-permute-done.2.west_ref
  27.4 2.1 %collective-permute-done.3.east_ref = bf16[160,128]{1,0:T(8,128)(2,1)S(1)} collective-permute-done((bf16[160,128]{1,0:T(8,128)(2,1)S(1)}, bf16[160,128]{1,0:T(8,128)(2,1)S(1)}, u32[]{:S(2)}, u32[]{:S(2)}) %collective-permute-start.3) | collective-permute-done | bytes 40992 | tf_op jit(solution)/shard_map/ppermute | solution.py:447
  29.6 0.0 copy-done.2
  29.6 0.0 copy-done.1
  29.6 0.0 copy-done
  29.6 0.0 copy-done.6
  29.6 0.0 copy-done.7
  29.6 0.0 copy-done.8
  29.6 22.0 %both_convs.1 = (bf16[16,32,32,128]{3,2,1,0:T(8,128)(2,1)S(1)}, bf16[8,32,32,128]{3,2,1,0:T(8,128)(2,1)S(1)}) custom-call(s32[2,8]{1,0:T(2,128)S(1)} %copy-done.4, s32[2,2,8]{2,1,0:T(2,128)S(1)} %bitcast.4, f32[32,1,128]{2,1,0:T(1,128)S(1)} %all-to-all-done.count_ref, bf16[2,8,32,32,128]{4,3,2,1,0:T(8,128)(2,1)} %fields_ref.3, ...), custom_call_target="tpu_custom_call" | custom-call | tf_op jit(solution)/shard_map/both_convs/pallas_call | solution.py:500
  51.7 2.7 %collective-permute-start.4 = (bf16[8,32,32,128]{3,2,1,0:T(8,128)(2,1)S(1)}, bf16[8,32,32,128]{3,2,1,0:T(8,128)(2,1)S(1)}, u32[]{:S(2)}, u32[]{:S(2)}) collective-permute-start(bf16[8,32,32,128]{3,2,1,0:T(8,128)(2,1)S(1)} %get-tuple-element.27), channel_id=1, source_target_pairs={{0,1},{1,0},{2,3},{3,2},{4,5},{5,4},{6,7},{7,6},{8,9},{9,8},{10,11... | collective-permute-start | bytes 6291464 | tf_op jit(solution)/shard_map/ppermute | solution.py:536
  54.4 3.8 %collective-permute-done.4.src_ref = bf16[8,32,32,128]{3,2,1,0:T(8,128)(2,1)S(1)} collective-permute-done((bf16[8,32,32,128]{3,2,1,0:T(8,128)(2,1)S(1)}, bf16[8,32,32,128]{3,2,1,0:T(8,128)(2,1)S(1)}, u32[]{:S(2)}, u32[]{:S(2)}) %collective-permute-start.4) | collective-permute-done | bytes 2097184 | tf_op jit(solution)/shard_map/ppermute | solution.py:536
  58.2 0.4 merge_mate.1
  58.5 0.0 copy-start.9
  58.6 58.9 %all_to_all.10.src_ref = bf16[16,32,32,128]{3,2,1,0:T(8,128)(2,1)S(1)} all-to-all(bf16[16,32,32,128]{3,2,1,0:T(8,128)(2,1)S(1)} %merge_mate.1), channel_id=1, replica_groups={{0,2,4,6,8,10,12,14,16,18,20,22,24,26,28,30},{1,3,5,7,9,11,13,15,17,19,..., dimensions={0} | all-to-all | bytes 8388608 | tf_op jit(solution)/shard_map/all_to_all | solution.py:548
  117.4 0.0 copy-done.9
  117.4 1.9 %slot_order.1 = bf16[8,32,32,128]{3,2,1,0:T(8,128)(2,1)} custom-call(s32[8]{0:T(128)S(1)} %copy-done.9, bf16[16,32,32,128]{3,2,1,0:T(8,128)(2,1)S(1)} %all_to_all.10.src_ref), custom_call_target="tpu_custom_call" | custom-call | tf_op jit(solution)/shard_map/slot_order/pallas_call | solution.py:551
Async XLA Ops:
  0.0 29.6 %copy-start.2 = (bf16[128,128]{1,0:T(8,128)(2,1)S(1)}, bf16[128,128]{1,0:T(8,128)(2,1)}, u32[]{:S(2)}) copy-start(bf16[128,128]{1,0:T(8,128)(2,1)} %mix_ref.1) | copy-start | bytes 98308
  0.0 29.6 %copy-start.1 = (bf16[3,3,128,128]{3,2,1,0:T(8,128)(2,1)S(1)}, bf16[3,3,128,128]{3,2,1,0:T(8,128)(2,1)}, u32[]{:S(2)}) copy-start(bf16[3,3,128,128]{3,2,1,0:T(8,128)(2,1)} %k2_ref.1) | copy-start | bytes 884740
  0.0 29.6 %copy-start = (bf16[3,3,128,128]{3,2,1,0:T(8,128)(2,1)S(1)}, bf16[3,3,128,128]{3,2,1,0:T(8,128)(2,1)}, u32[]{:S(2)}) copy-start(bf16[3,3,128,128]{3,2,1,0:T(8,128)(2,1)} %k1_ref.1) | copy-start | bytes 884740
  0.0 0.7 copy-start.3
  0.8 0.7 copy-start.5
  1.4 15.7 %copy-start.4 = (s32[2,8]{1,0:T(2,128)S(1)}, s32[2,8]{1,0:T(2,128)}, u32[]{:S(2)}) copy-start(s32[2,8]{1,0:T(2,128)} %wet_ref.5) | copy-start | bytes 196
  1.4 28.2 %copy-start.6 = (s32[2,8,2]{1,2,0:T(2,128)S(1)}, s32[2,8,2]{1,2,0:T(2,128)}, u32[]{:S(2)}) copy-start(s32[2,8,2]{1,2,0:T(2,128)} %param.11) | copy-start | bytes 388
  1.4 28.2 %copy-start.7 = (f32[128]{0:T(128)S(1)}, f32[128]{0:T(128)}, u32[]{:S(2)}) copy-start(f32[128]{0:T(128)} %param.14) | copy-start | bytes 1540
  1.4 28.2 %copy-start.8 = (f32[128]{0:T(128)S(1)}, f32[128]{0:T(128)}, u32[]{:S(2)}) copy-start(f32[128]{0:T(128)} %param.16) | copy-start | bytes 1540
  3.9 13.2 %collective-permute-start = (bf16[528,128]{1,0:T(8,128)(2,1)S(1)}, bf16[528,128]{1,0:T(8,128)(2,1)S(1)}, u32[]{:S(2)}, u32[]{:S(2)}) collective-permute-start(bf16[528,128]{1,0:T(8,128)(2,1)S(1)} %get-tuple-element.17), channel_id=1, source_target_pairs={{0,32},{32,64},{64,96},{1,33},{33,65},{65,97},{2,34},{34,66},{66,9... | collective-permute-start | bytes 405512 | tf_op jit(solution)/shard_map/ppermute | solution.py:447
  7.7 9.4 %collective-permute-start.1 = (bf16[528,128]{1,0:T(8,128)(2,1)S(1)}, bf16[528,128]{1,0:T(8,128)(2,1)S(1)}, u32[]{:S(2)}, u32[]{:S(2)}) collective-permute-start(bf16[528,128]{1,0:T(8,128)(2,1)S(1)} %get-tuple-element.18), channel_id=1, source_target_pairs={{32,0},{64,32},{96,64},{33,1},{65,33},{97,65},{34,2},{66,34},{98,6... | collective-permute-start | bytes 405512 | tf_op jit(solution)/shard_map/ppermute | solution.py:447
  9.7 14.6 %all-to-all-start = ((f32[32,1,128]{2,1,0:T(1,128)}), f32[32,1,128]{2,1,0:T(1,128)S(1)}, u32[]{:S(2)}, u32[]{:S(2)}) async-start(f32[32,1,128]{2,1,0:T(1,128)} %get-tuple-element.23), calls=%async_computation | async-start | bytes 32768 | tf_op jit(solution)/shard_map/all_to_all | solution.py:482
  24.4 3.1 %collective-permute-start.2 = (bf16[160,128]{1,0:T(8,128)(2,1)S(1)}, bf16[160,128]{1,0:T(8,128)(2,1)S(1)}, u32[]{:S(2)}, u32[]{:S(2)}) collective-permute-start(bf16[160,128]{1,0:T(8,128)(2,1)S(1)} %get-tuple-element.25), channel_id=1, source_target_pairs={{0,1},{1,2},{2,3},{3,4},{4,5},{5,6},{6,7},{7,8},{8,9},{9,10},{10,1... | collective-permute-start | bytes 122888 | tf_op jit(solution)/shard_map/ppermute | solution.py:447
  26.1 3.5 %collective-permute-start.3 = (bf16[160,128]{1,0:T(8,128)(2,1)S(1)}, bf16[160,128]{1,0:T(8,128)(2,1)S(1)}, u32[]{:S(2)}, u32[]{:S(2)}) collective-permute-start(bf16[160,128]{1,0:T(8,128)(2,1)S(1)} %get-tuple-element.26), channel_id=1, source_target_pairs={{1,0},{2,1},{3,2},{4,3},{5,4},{6,5},{7,6},{8,7},{9,8},{10,9},{11,1... | collective-permute-start | bytes 122888 | tf_op jit(solution)/shard_map/ppermute | solution.py:447
  51.7 6.5 %collective-permute-start.4 = (bf16[8,32,32,128]{3,2,1,0:T(8,128)(2,1)S(1)}, bf16[8,32,32,128]{3,2,1,0:T(8,128)(2,1)S(1)}, u32[]{:S(2)}, u32[]{:S(2)}) collective-permute-start(bf16[8,32,32,128]{3,2,1,0:T(8,128)(2,1)S(1)} %get-tuple-element.27), channel_id=1, source_target_pairs={{0,1},{1,0},{2,3},{3,2},{4,5},{5,4},{6,7},{7,6},{8,9},{9,8},{10,11... | collective-permute-start | bytes 6291464 | tf_op jit(solution)/shard_map/ppermute | solution.py:536
  58.5 58.9 %copy-start.9 = (s32[8]{0:T(128)S(1)}, s32[8]{0:T(128)}, u32[]{:S(2)}) copy-start(s32[8]{0:T(128)} %list_ref.1) | copy-start | bytes 100

commit v3 on v2

--- a/solution.py
+++ b/solution.py
@@ -9,7 +9,7 @@
 
 F32 = jnp.float32
 BF16 = jnp.bfloat16
-VMEM_LIMIT = 32 * 1024 * 1024
+VMEM_LIMIT = 26 * 1024 * 1024
 WHOLE = pl.BlockSpec(memory_space=pltpu.VMEM)
 SCALARS = pl.BlockSpec(memory_space=pltpu.SMEM)
 IN_PLACE = pl.BlockSpec(memory_space=pl.ANY)
@@ -199,11 +199,63 @@
     return jnp.max(jnp.sum(earlier, axis=0)).astype(jnp.int32)
 
 
-def conv_kernel(
-    wet_ref, seam_ref, count_ref, fields_ref, north_ref, south_ref, west_ref, east_ref,
-    lcol_ref, rcol_ref, k1_ref, b1_ref, k2_ref, b2_ref, mix_ref, keep_ref, give_ref,
-    own_tiles, out_ref, x_ref, hid_ref, br_ref, w1_ref, w2_ref, mm_ref, m_ref, pack_ref, own_ref, ext_ref, t_ref,
-    zw1_ref, ze1_ref, zw2_ref, ze2_ref, in_sems, sems,
+def first_kernel(
+    wet_ref, fields_ref, k_ref, b_ref, made_ref, col_ref, row_ref,
+    own_tiles, x_ref, hid_ref, w_ref, m_ref, in_sems, out_sems,
+):
+    tr_dev, tc_dev, tile, _, ch = fields_ref.shape
+    width, height = tc_dev * tile, tr_dev * tile
+    loads = [
+        pltpu.make_async_copy(fields_ref.at[i], own_tiles.at[i], in_sems.at[i])
+        for i in range(tr_dev)
+    ]
+    for load in loads:
+        load.start()
+    fill_weights(k_ref, w_ref)
+    bias = b_ref[...]
+    x_ref[0] = jnp.zeros((width, ch), BF16)
+    x_ref[height + 1] = jnp.zeros((width, ch), BF16)
+    nothing = jnp.zeros((1, ch), F32)
+    stores = []
+
+    def store(n, row):
+        rows = slice(row, row + tile // 2)
+        return pltpu.make_async_copy(hid_ref.at[rows], made_ref.at[rows], out_sems.at[n])
+
+    done = 0
+    for i in range(tr_dev):
+        loads[i].wait()
+        for j in range(tc_dev):
+            scale = jnp.full((1, ch), 1.0, F32) * wet_ref[i, j].astype(F32)
+            m_ref[i, j * tile : (j + 1) * tile] = jnp.broadcast_to(scale, (tile, ch))
+            x_ref[1 + i * tile : 1 + (i + 1) * tile, j * tile : (j + 1) * tile] = (
+                own_tiles[i, j] * scale.astype(BF16)[None]
+            )
+        ready = (i + 1) * tile // 2 - (i < tr_dev - 1)
+        for row in range(2 * done, 2 * ready, 2):
+            z = dot(jnp.concatenate([x_ref[row + n] for n in range(4)], axis=1), w_ref[...])
+            for ro in range(2):
+                total = side_sums(z, 3 * ro * ch, nothing, nothing) + bias
+                col_ref[0, row + ro : row + ro + 1] = total[0:1]
+                col_ref[1, row + ro : row + ro + 1] = total[width - 1 : width]
+                if row + ro == 0:
+                    row_ref[0] = total
+                if row + ro == height - 1:
+                    row_ref[1] = total
+                hid_ref[row + ro] = (gelu(total) * m_ref[row // tile]).astype(BF16)
+            if (row + 2) % (tile // 2) == 0:
+                stores.append(store(len(stores), row + 2 - tile // 2))
+                stores[-1].start()
+        done = ready
+    for copy in stores:
+        copy.wait()
+
+
+def second_kernel(
+    wet_ref, seam_ref, count_ref, fields_ref, made_ref, col_ref, row_ref, top_ref, bottom_ref,
+    north_ref, south_ref, west_ref, east_ref, lcol_ref, rcol_ref, k1_ref, b1_ref, k2_ref, b2_ref, mix_ref, keep_ref, give_ref,
+    own_tiles, out_ref, hid_ref, br_ref, w1_ref, w2_ref, mm_ref, pack_ref, own_ref, ext_ref, t_ref,
+    zw1_ref, ze1_ref, zw2_ref, ze2_ref, hid_sem, in_sems, sems,
 ):
     tr_dev, tc_dev, tile, _, ch = fields_ref.shape
     width, height = tc_dev * tile, tr_dev * tile
@@ -213,9 +265,11 @@
     loads = [
         pltpu.make_async_copy(fields_ref.at[i], own_tiles.at[i], in_sems.at[i]) for i in range(tr_dev)
     ]
-    for load in loads:
-        load.start()
-    fill_weights(k1_ref, w1_ref)
+    hid_load = pltpu.make_async_copy(made_ref, hid_ref.at[1 : height + 1], hid_sem)
+    hid_load.start()
+    for dy in range(3):
+        for dx in range(3):
+            w1_ref[dy * ch : (dy + 1) * ch, dx * ch : (dx + 1) * ch] = k1_ref[dy, dx]
     fill_weights(k2_ref, w2_ref)
     zero = jnp.zeros((ch, ch), BF16)
     mm_ref[:ch, :ch] = mix_ref[...]
@@ -292,26 +346,17 @@
         z_ref = (zw2_ref, ze2_ref)[s]
         z_ref[0:lines] = tall_conv(t_ref.at[0], k2_ref, 2 * s, lines)
 
-    x_ref[0] = north_ref[width : 2 * width]
-    x_ref[height + 1] = south_ref[0:width]
-
-    def fill(i):
-        loads[i].wait()
-        for j in range(tc_dev):
-            scale = jnp.full((1, ch), 1.0, F32) * wet_ref[i, j].astype(F32)
-            m_ref[i, j * tile : (j + 1) * tile] = jnp.broadcast_to(scale, (tile, ch))
-            x_ref[1 + i * tile : 1 + (i + 1) * tile, j * tile : (j + 1) * tile] = (
-                own_tiles[i, j] * scale.astype(BF16)[None]
-            )
-
     beyond = (
-        (0, [north_ref.at[0:width], north_ref.at[width : 2 * width], x_ref.at[1]], 0, notes[0]),
-        (height + 1, [x_ref.at[height], south_ref.at[0:width], south_ref.at[width : 2 * width]], lines - 1, notes[1]),
+        (0, [north_ref[0:width], north_ref[width : 2 * width], top_ref[0:width]], 0, notes[0]),
+        (
+            height + 1,
+            [bottom_ref[width : 2 * width], south_ref[0:width], south_ref[width : 2 * width]],
+            lines - 1,
+            notes[1],
+        ),
     )
-
-    def outside(row, window, line, note):
-        window = [w[...] for w in window]
-        z = dot(jnp.concatenate(window, axis=1), w1_ref[: 3 * ch, : 3 * ch])
+    for row, window, line, note in beyond:
+        z = dot(jnp.concatenate(window, axis=1), w1_ref[...])
         total = side_sums(z, 0, zw1_ref[line : line + 1], ze1_ref[line : line + 1]) + bias1
         value = gelu(total)
         for j in range(tc_dev):
@@ -319,13 +364,32 @@
                 value[j * tile : (j + 1) * tile] * note[4 + j : 5 + j]
             ).astype(BF16)
 
-    def first(p, carry):
-        row = 2 * p
-        window = [x_ref[row + k] for k in range(4)]
-        outs = conv_pair(window, w1_ref, bias1, zw1_ref, ze1_ref, line_at(row, tile))
-        for ro in range(2):
-            hid_ref[1 + row + ro] = (gelu(outs[ro]) * m_ref[row // tile]).astype(BF16)
-        return carry
+    hid_load.wait()
+    for load in loads:
+        load.start()
+    part = 16
+    for s in range(2):
+        z_ref = (zw1_ref, ze1_ref)[s]
+        at = s * (width - part)
+        place_in = lax.broadcasted_iota(jnp.int32, (tile, part, ch), 1)
+        for i in range(tr_dev):
+            line = line_at(i * tile, tile)
+            total = col_ref[s, i * tile : (i + 1) * tile] + z_ref[line : line + tile]
+            value = gelu(total) * wet_ref[i, s * (tc_dev - 1)].astype(F32)
+            held = hid_ref[1 + i * tile : 1 + (i + 1) * tile, at : at + part].astype(F32)
+            fixed = jnp.where(place_in == s * (part - 1), value[:, None, :], held)
+            hid_ref[1 + i * tile : 1 + (i + 1) * tile, at : at + part] = fixed.astype(BF16)
+    for n, outer in enumerate((north_ref[width : 2 * width], south_ref[0:width])):
+        row = n * (height - 1)
+        line = line_at(row, tile)
+        z = dot(outer, w1_ref[2 * n * ch : (2 * n + 1) * ch])
+        total = row_ref[n] + side_sums(z, 0, zw1_ref[line : line + 1], ze1_ref[line : line + 1])
+        value = gelu(total)
+        for j in range(tc_dev):
+            wet = wet_ref[row // tile, j].astype(F32)
+            hid_ref[1 + row, j * tile : (j + 1) * tile] = (
+                value[j * tile : (j + 1) * tile] * wet
+            ).astype(BF16)
 
     def branch(p):
         row = 2 * p
@@ -387,18 +451,9 @@
             def _():
                 pltpu.make_async_copy(out_ref.at[i, j], keep_ref.at[0], sems.at[k]).wait()
 
-    done = 0
-    for i in range(tr_dev):
-        fill(i)
-        if i == 0:
-            outside(*beyond[0])
-        if i == tr_dev - 1:
-            outside(*beyond[1])
-        ready = (i + 1) * tile // 2 - (i < tr_dev - 1)
-        lax.fori_loop(done, ready, first, 0, unroll=ready - done)
-        done = ready
     for i in range(tr_dev):
         lax.fori_loop(i * tile // 2, (i + 1) * tile // 2, second, 0, unroll=tile // 2)
+        loads[i].wait()
         lax.fori_loop(i * tile // 2, (i + 1) * tile // 2, third, 0, unroll=8)
         start_copies(i)
     for i in range(tr_dev):
@@ -457,9 +512,10 @@
     chips = columns // 2
     width, height = tc_dev * tile, tr_dev * tile
     half = face // 2
-    seams = jnp.swapaxes(seam_flags, 1, 2)
+    seams = pltpu.with_memory_space_constraint(jnp.swapaxes(seam_flags, 1, 2), pltpu.HBM)
+    wet_mask = pltpu.with_memory_space_constraint(wet_mask, pltpu.HBM)
     params = pltpu.CompilerParams(vmem_limit_bytes=VMEM_LIMIT)
-    small = pltpu.CompilerParams(vmem_limit_bytes=VMEM_LIMIT // 8)
+    small = pltpu.CompilerParams(vmem_limit_bytes=VMEM_LIMIT // 6)
     fields = pltpu.with_memory_space_constraint(fields, pltpu.HBM)
     strip = jax.ShapeDtypeStruct((2 * width + 16, ch), BF16)
     pair = jax.ShapeDtypeStruct((2, height, ch), BF16)
@@ -490,31 +546,52 @@
         compiler_params=small,
         name="side",
     )(wet_mask, north, south, lcols, rcols)
-    left, right, counts = lax.optimization_barrier((left, right, counts))
-    west = shifted(right, "col", 1)
-    east = shifted(left, "col", -1)
 
     tile_shape = (tile, tile, ch)
     lines = 8 + (tile + 2) * tr_dev
     lines += -lines % 8
+    hid, edge_cols, edge_rows = pl.pallas_call(
+        first_kernel,
+        out_shape=(
+            pltpu.HBM((height, width, ch), BF16),
+            jax.ShapeDtypeStruct((2, height, ch), F32),
+            jax.ShapeDtypeStruct((2, width, ch), F32),
+        ),
+        in_specs=[SCALARS, IN_HBM, WHOLE, WHOLE],
+        out_specs=(IN_HBM, WHOLE, WHOLE),
+        scratch_shapes=[
+            pltpu.VMEM(fields.shape, BF16),
+            pltpu.VMEM((height + 2, width, ch), BF16),
+            pltpu.VMEM((height, width, ch), BF16),
+            pltpu.VMEM((4 * ch, 6 * ch), BF16),
+            pltpu.VMEM((tr_dev, width, ch), F32),
+            pltpu.SemaphoreType.DMA((tr_dev,)),
+            pltpu.SemaphoreType.DMA((2 * tr_dev,)),
+        ],
+        compiler_params=params,
+        name="first_conv",
+    )(wet_mask, fields, kernel_one, bias_one[None])
+
+    hid = pltpu.with_memory_space_constraint(hid, pltpu.HBM)
+    left, right, counts, edge_rows = lax.optimization_barrier((left, right, counts, edge_rows))
+    west = shifted(right, "col", 1)
+    east = shifted(left, "col", -1)
     keep, give = pl.pallas_call(
-        conv_kernel,
+        second_kernel,
         out_shape=(
             jax.ShapeDtypeStruct((chips,) + tile_shape, BF16),
             jax.ShapeDtypeStruct((half,) + tile_shape, BF16),
         ),
-        in_specs=[SCALARS, SCALARS, WHOLE, IN_HBM] + [WHOLE] * 11,
+        in_specs=[SCALARS, SCALARS, WHOLE, IN_HBM, IN_HBM] + [WHOLE] * 15,
         out_specs=(IN_PLACE, IN_PLACE),
         scratch_shapes=[
             pltpu.VMEM(fields.shape, BF16),
             pltpu.VMEM(fields.shape, BF16),
             pltpu.VMEM((height + 2, width, ch), BF16),
-            pltpu.VMEM((height + 2, width, ch), BF16),
             pltpu.VMEM((height // 2, width, 2 * ch), BF16),
-            pltpu.VMEM((4 * ch, 6 * ch), BF16),
+            pltpu.VMEM((3 * ch, 3 * ch), BF16),
             pltpu.VMEM((4 * ch, 6 * ch), BF16),
             pltpu.VMEM((2 * ch, 2 * ch), BF16),
-            pltpu.VMEM((tr_dev, width, ch), F32),
             pltpu.VMEM((2,) + west.shape, F32),
             pltpu.VMEM((2, height + 8, ch), F32),
             pltpu.VMEM((2, height + 8, ch), F32),
@@ -523,13 +600,15 @@
             pltpu.VMEM((lines, ch), F32),
             pltpu.VMEM((lines, ch), F32),
             pltpu.VMEM((lines, ch), F32),
+            pltpu.SemaphoreType.DMA,
             pltpu.SemaphoreType.DMA((tr_dev,)),
             pltpu.SemaphoreType.DMA((face,)),
         ],
         compiler_params=params,
-        name="both_convs",
+        name="second_conv",
     )(
-        wet_mask, seams, counts, fields, north, south, west, east, lcols, rcols,
+        wet_mask, seams, counts, fields, hid, edge_cols, edge_rows, top, bottom,
+        north, south, west, east, lcols, rcols,
         kernel_one, bias_one[None], kernel_two, bias_two[None], mixing,
     )
 

time: 120 us -> 120 us (level)
  waiting for transfers between devices: 12.6 us -> 6.55 us
  Pallas kernels: 27.4 us -> 33.4 us
  local copies, waits for them, and re-layouts: 1.45 us -> 0.03 us
    all_to_all x1, waiting for transfers between devices: 6.67 us -> 0.01 us  [on_device(): lax.all_to_all(count, 'col', split_axis=0, concat_axis=0, tiled=True)]
    pallas_call x1 -> x2, Pallas kernels: 22 us -> 27.8 us  [the longest x1 15.4 us: on_device(): pl.pallas_call(second_kernel, out_shape=(jax.ShapeDtypeStruct((chips,) +...]
    unnamed x20 -> x12, local copies, waits for them, and re-layouts: 1.45 us -> 0.03 us
  transfers between devices with their start and end apart: 6 -> 6, of which waited for: 3 -> 2; matrix products, arithmetic and copies ran while one was open for 0% -> 0% of each run, Pallas kernels for 0% -> 11%
where the time goes in v3:
time: 120 us; the launch traced here: 119 us
  blocking collectives  59.7 us (50%)
  Pallas kernels  33.4 us (28%)
  starting transfers between devices  19.3 us (16%)
  waiting for transfers between devices  6.55 us (5%)
    all_to_all x1, blocking collectives, on_device(): lax.all_to_all(sending, 'col', split_axis=0, concat_axis=0, tiled=True, a...  59.7 us
    pallas_call x1, Pallas kernels, on_device(): pl.pallas_call(second_kernel, out_shape=(jax.ShapeDtypeStruct((chips,) +...  15.4 us
    pallas_call x1, Pallas kernels, on_device(): pl.pallas_call(first_kernel, out_shape=(pltpu.HBM((height, width, ch), BF...  12.3 us
    ppermute x4, starting transfers between devices, shifted(): return lax.ppermute(x, axis, pairs)  9.47 us
    all_to_all x1, starting transfers between devices, on_device(): lax.all_to_all(count, 'col', split_axis=0, concat_axis=0, tiled=True)  7.33 us
    ppermute x1, waiting for transfers between devices, on_device(): taken = lax.ppermute(give, 'col', [(i, i ^ 1) for i in range(columns)])  3.79 us
    ppermute x4, waiting for transfers between devices, shifted(): return lax.ppermute(x, axis, pairs)  2.76 us
    pallas_call x1, Pallas kernels, on_device(): pl.pallas_call(rim_kernel, out_shape=(strip, strip, pair, pair, jax.Shape...  2.69 us
  transfers between devices with their start and end apart: 6, of which 2 were waited for; matrix products, arithmetic and copies ran while one was open for 0% of the time, Pallas kernels for 11%

profile of v3, /device:TPU:32, one launch (start us, length us, event | category | flops | bytes accessed | tf_op | source)
XLA Modules:
  0.0 119.4 jit_solution(10398412831176727815)
XLA Ops:
  0.0 0.0 copy-start
  0.0 0.0 copy-start.3
  0.0 0.0 copy-start.1
  0.0 0.0 copy-start.2
  0.0 0.0 copy-start.4
  0.0 2.7 %rim.1 = (bf16[528,128]{1,0:T(8,128)(2,1)S(1)}, bf16[528,128]{1,0:T(8,128)(2,1)S(1)}, bf16[2,64,128]{2,1,0:T(8,128)(2,1)S(1)}, bf16[2,64,128]{2,1,0:T(8,128)(2,1)S(1)}, f32[32,1,128]{2,1,0:T(1,128)}) custom-call(s32[2,8]{1,0:T(2,128)} %wet_ref.7, s32[2,2,8]{2,1,0:T(2,128)} %bitcast.6, bf16[2,8,32,32,128]{4,3,2,1,0:T(8,128)(2,1)} %fields_ref.5), custom_call_target="tpu_custom_call" | custom-call | tf_op jit(solution)/shard_map/rim/pallas_call | solution.py:522
  2.7 3.8 %collective-permute-start = (bf16[528,128]{1,0:T(8,128)(2,1)S(1)}, bf16[528,128]{1,0:T(8,128)(2,1)S(1)}, u32[]{:S(2)}, u32[]{:S(2)}) collective-permute-start(bf16[528,128]{1,0:T(8,128)(2,1)S(1)} %get-tuple-element.21.bottom_ref), channel_id=1, source_target_pairs={{0,32},{32,64},{64,96},{1,33},{33,65},{65,97},{2,34},{34,66},{66,9... | collective-permute-start | bytes 405512 | tf_op jit(solution)/shard_map/ppermute | solution.py:502
  6.6 2.0 %collective-permute-start.1 = (bf16[528,128]{1,0:T(8,128)(2,1)S(1)}, bf16[528,128]{1,0:T(8,128)(2,1)S(1)}, u32[]{:S(2)}, u32[]{:S(2)}) collective-permute-start(bf16[528,128]{1,0:T(8,128)(2,1)S(1)} %get-tuple-element.22.top_ref), channel_id=1, source_target_pairs={{32,0},{64,32},{96,64},{33,1},{65,33},{97,65},{34,2},{66,34},{98,6... | collective-permute-start | bytes 405512 | tf_op jit(solution)/shard_map/ppermute | solution.py:502
  8.6 7.3 %all-to-all-start = ((f32[32,1,128]{2,1,0:T(1,128)}), f32[32,1,128]{2,1,0:T(1,128)S(1)}, u32[]{:S(2)}, u32[]{:S(2)}) async-start(f32[32,1,128]{2,1,0:T(1,128)} %get-tuple-element.27), calls=%async_computation | async-start | bytes 32768 | tf_op jit(solution)/shard_map/all_to_all | solution.py:538
  15.9 0.0 copy-done
  15.9 0.0 copy-done.3
  15.9 12.3 %first_conv.1 = (bf16[64,256,128]{2,1,0:T(8,128)(2,1)}, f32[2,64,128]{2,1,0:T(8,128)S(1)}, f32[2,256,128]{2,1,0:T(8,128)S(1)}) custom-call(s32[2,8]{1,0:T(2,128)} %wet_ref.7, bf16[2,8,32,32,128]{4,3,2,1,0:T(8,128)(2,1)} %fields_ref.5, bf16[3,3,128,128]{3,2,1,0:T(8,128)(2,1)S(1)} %copy-done, f32[1,128]{1,0:T(1,128)S(1)} %bitcast.3), custom_call_target="tpu_custom_call" | custom-call | tf_op jit(solution)/shard_map/first_conv/pallas_call | solution.py:553
  28.3 0.0 collective-permute-done.north_ref
  28.3 0.0 collective-permute-done.1.south_ref
  28.3 0.7 side.1
  29.1 0.0 all-to-all-done.count_ref
  29.1 2.2 %collective-permute-start.2 = (bf16[160,128]{1,0:T(8,128)(2,1)S(1)}, bf16[160,128]{1,0:T(8,128)(2,1)S(1)}, u32[]{:S(2)}, u32[]{:S(2)}) collective-permute-start(bf16[160,128]{1,0:T(8,128)(2,1)S(1)} %get-tuple-element.33), channel_id=1, source_target_pairs={{0,1},{1,2},{2,3},{3,4},{4,5},{5,6},{6,7},{7,8},{8,9},{9,10},{10,1... | collective-permute-start | bytes 122888 | tf_op jit(solution)/shard_map/ppermute | solution.py:502
  31.2 1.5 %collective-permute-start.3 = (bf16[160,128]{1,0:T(8,128)(2,1)S(1)}, bf16[160,128]{1,0:T(8,128)(2,1)S(1)}, u32[]{:S(2)}, u32[]{:S(2)}) collective-permute-start(bf16[160,128]{1,0:T(8,128)(2,1)S(1)} %get-tuple-element.34), channel_id=1, source_target_pairs={{1,0},{2,1},{3,2},{4,3},{5,4},{6,5},{7,6},{8,7},{9,8},{10,9},{11,1... | collective-permute-start | bytes 122888 | tf_op jit(solution)/shard_map/ppermute | solution.py:502
  32.7 0.0 collective-permute-done.2.west_ref
  32.7 2.8 %collective-permute-done.3.east_ref = bf16[160,128]{1,0:T(8,128)(2,1)S(1)} collective-permute-done((bf16[160,128]{1,0:T(8,128)(2,1)S(1)}, bf16[160,128]{1,0:T(8,128)(2,1)S(1)}, u32[]{:S(2)}, u32[]{:S(2)}) %collective-permute-start.3) | collective-permute-done | bytes 40992 | tf_op jit(solution)/shard_map/ppermute | solution.py:502
  35.5 0.0 copy-done.1
  35.5 0.0 copy-done.2
  35.5 0.0 copy-done.4
  35.5 15.4 %second_conv.1 = (bf16[16,32,32,128]{3,2,1,0:T(8,128)(2,1)S(1)}, bf16[8,32,32,128]{3,2,1,0:T(8,128)(2,1)S(1)}) custom-call(s32[2,8]{1,0:T(2,128)} %wet_ref.7, s32[2,2,8]{2,1,0:T(2,128)} %bitcast.7, f32[32,1,128]{2,1,0:T(1,128)S(1)} %all-to-all-done.count_ref, bf16[2,8,32,32,128]{4,3,2,1,0:T(8,128)(2,1)} %fields_ref.5, ...), custom_call_target="tpu_custom_call" | custom-call | tf_op jit(solution)/shard_map/second_conv/pallas_call | solution.py:579
  50.9 2.5 %collective-permute-start.4 = (bf16[8,32,32,128]{3,2,1,0:T(8,128)(2,1)S(1)}, bf16[8,32,32,128]{3,2,1,0:T(8,128)(2,1)S(1)}, u32[]{:S(2)}, u32[]{:S(2)}) collective-permute-start(bf16[8,32,32,128]{3,2,1,0:T(8,128)(2,1)S(1)} %get-tuple-element.35), channel_id=1, source_target_pairs={{0,1},{1,0},{2,3},{3,2},{4,5},{5,4},{6,7},{7,6},{8,9},{9,8},{10,11... | collective-permute-start | bytes 6291464 | tf_op jit(solution)/shard_map/ppermute | solution.py:615
  53.4 3.8 %collective-permute-done.4.src_ref = bf16[8,32,32,128]{3,2,1,0:T(8,128)(2,1)S(1)} collective-permute-done((bf16[8,32,32,128]{3,2,1,0:T(8,128)(2,1)S(1)}, bf16[8,32,32,128]{3,2,1,0:T(8,128)(2,1)S(1)}, u32[]{:S(2)}, u32[]{:S(2)}) %collective-permute-start.4) | collective-permute-done | bytes 2097184 | tf_op jit(solution)/shard_map/ppermute | solution.py:615
  57.2 0.3 merge_mate.1
  57.5 0.0 copy-start.5
  57.5 59.7 %all_to_all.10.src_ref = bf16[16,32,32,128]{3,2,1,0:T(8,128)(2,1)S(1)} all-to-all(bf16[16,32,32,128]{3,2,1,0:T(8,128)(2,1)S(1)} %merge_mate.1), channel_id=1, replica_groups={{0,2,4,6,8,10,12,14,16,18,20,22,24,26,28,30},{1,3,5,7,9,11,13,15,17,19,..., dimensions={0} | all-to-all | bytes 8388608 | tf_op jit(solution)/shard_map/all_to_all | solution.py:627
  117.3 0.0 copy-done.5
  117.3 1.9 %slot_order.1 = bf16[8,32,32,128]{3,2,1,0:T(8,128)(2,1)} custom-call(s32[8]{0:T(128)S(1)} %copy-done.5, bf16[16,32,32,128]{3,2,1,0:T(8,128)(2,1)S(1)} %all_to_all.10.src_ref), custom_call_target="tpu_custom_call" | custom-call | tf_op jit(solution)/shard_map/slot_order/pallas_call | solution.py:630
Async XLA Ops:
  0.0 15.9 %copy-start = (bf16[3,3,128,128]{3,2,1,0:T(8,128)(2,1)S(1)}, bf16[3,3,128,128]{3,2,1,0:T(8,128)(2,1)}, u32[]{:S(2)}) copy-start(bf16[3,3,128,128]{3,2,1,0:T(8,128)(2,1)} %k1_ref.1) | copy-start | bytes 884740
  0.0 15.9 %copy-start.3 = (f32[128]{0:T(128)S(1)}, f32[128]{0:T(128)}, u32[]{:S(2)}) copy-start(f32[128]{0:T(128)} %param.14) | copy-start | bytes 1540
  0.0 35.5 %copy-start.1 = (bf16[3,3,128,128]{3,2,1,0:T(8,128)(2,1)S(1)}, bf16[3,3,128,128]{3,2,1,0:T(8,128)(2,1)}, u32[]{:S(2)}) copy-start(bf16[3,3,128,128]{3,2,1,0:T(8,128)(2,1)} %k2_ref.1) | copy-start | bytes 884740
  0.0 35.5 %copy-start.2 = (bf16[128,128]{1,0:T(8,128)(2,1)S(1)}, bf16[128,128]{1,0:T(8,128)(2,1)}, u32[]{:S(2)}) copy-start(bf16[128,128]{1,0:T(8,128)(2,1)} %mix_ref.1) | copy-start | bytes 98308
  0.0 35.5 %copy-start.4 = (f32[128]{0:T(128)S(1)}, f32[128]{0:T(128)}, u32[]{:S(2)}) copy-start(f32[128]{0:T(128)} %param.16) | copy-start | bytes 1540
  2.7 25.6 %collective-permute-start = (bf16[528,128]{1,0:T(8,128)(2,1)S(1)}, bf16[528,128]{1,0:T(8,128)(2,1)S(1)}, u32[]{:S(2)}, u32[]{:S(2)}) collective-permute-start(bf16[528,128]{1,0:T(8,128)(2,1)S(1)} %get-tuple-element.21.bottom_ref), channel_id=1, source_target_pairs={{0,32},{32,64},{64,96},{1,33},{33,65},{65,97},{2,34},{34,66},{66,9... | collective-permute-start | bytes 405512 | tf_op jit(solution)/shard_map/ppermute | solution.py:502
  6.6 21.8 %collective-permute-start.1 = (bf16[528,128]{1,0:T(8,128)(2,1)S(1)}, bf16[528,128]{1,0:T(8,128)(2,1)S(1)}, u32[]{:S(2)}, u32[]{:S(2)}) collective-permute-start(bf16[528,128]{1,0:T(8,128)(2,1)S(1)} %get-tuple-element.22.top_ref), channel_id=1, source_target_pairs={{32,0},{64,32},{96,64},{33,1},{65,33},{97,65},{34,2},{66,34},{98,6... | collective-permute-start | bytes 405512 | tf_op jit(solution)/shard_map/ppermute | solution.py:502
  8.6 20.5 %all-to-all-start = ((f32[32,1,128]{2,1,0:T(1,128)}), f32[32,1,128]{2,1,0:T(1,128)S(1)}, u32[]{:S(2)}, u32[]{:S(2)}) async-start(f32[32,1,128]{2,1,0:T(1,128)} %get-tuple-element.27), calls=%async_computation | async-start | bytes 32768 | tf_op jit(solution)/shard_map/all_to_all | solution.py:538
  29.1 3.6 %collective-permute-start.2 = (bf16[160,128]{1,0:T(8,128)(2,1)S(1)}, bf16[160,128]{1,0:T(8,128)(2,1)S(1)}, u32[]{:S(2)}, u32[]{:S(2)}) collective-permute-start(bf16[160,128]{1,0:T(8,128)(2,1)S(1)} %get-tuple-element.33), channel_id=1, source_target_pairs={{0,1},{1,2},{2,3},{3,4},{4,5},{5,6},{6,7},{7,8},{8,9},{9,10},{10,1... | collective-permute-start | bytes 122888 | tf_op jit(solution)/shard_map/ppermute | solution.py:502
  31.2 4.2 %collective-permute-start.3 = (bf16[160,128]{1,0:T(8,128)(2,1)S(1)}, bf16[160,128]{1,0:T(8,128)(2,1)S(1)}, u32[]{:S(2)}, u32[]{:S(2)}) collective-permute-start(bf16[160,128]{1,0:T(8,128)(2,1)S(1)} %get-tuple-element.34), channel_id=1, source_target_pairs={{1,0},{2,1},{3,2},{4,3},{5,4},{6,5},{7,6},{8,7},{9,8},{10,9},{11,1... | collective-permute-start | bytes 122888 | tf_op jit(solution)/shard_map/ppermute | solution.py:502
  50.9 6.3 %collective-permute-start.4 = (bf16[8,32,32,128]{3,2,1,0:T(8,128)(2,1)S(1)}, bf16[8,32,32,128]{3,2,1,0:T(8,128)(2,1)S(1)}, u32[]{:S(2)}, u32[]{:S(2)}) collective-permute-start(bf16[8,32,32,128]{3,2,1,0:T(8,128)(2,1)S(1)} %get-tuple-element.35), channel_id=1, source_target_pairs={{0,1},{1,0},{2,3},{3,2},{4,5},{5,4},{6,7},{7,6},{8,9},{9,8},{10,11... | collective-permute-start | bytes 6291464 | tf_op jit(solution)/shard_map/ppermute | solution.py:615
  57.5 59.7 %copy-start.5 = (s32[8]{0:T(128)S(1)}, s32[8]{0:T(128)}, u32[]{:S(2)}) copy-start(s32[8]{0:T(128)} %list_ref.1) | copy-start | bytes 100

commit v4 on v2

--- a/solution.py
+++ b/solution.py
@@ -457,7 +457,8 @@
     chips = columns // 2
     width, height = tc_dev * tile, tr_dev * tile
     half = face // 2
-    seams = jnp.swapaxes(seam_flags, 1, 2)
+    seams = pltpu.with_memory_space_constraint(jnp.swapaxes(seam_flags, 1, 2), pltpu.HBM)
+    wet_mask = pltpu.with_memory_space_constraint(wet_mask, pltpu.HBM)
     params = pltpu.CompilerParams(vmem_limit_bytes=VMEM_LIMIT)
     small = pltpu.CompilerParams(vmem_limit_bytes=VMEM_LIMIT // 8)
     fields = pltpu.with_memory_space_constraint(fields, pltpu.HBM)

time: 120 us -> 119 us (level)
  local copies, waits for them, and re-layouts: 1.45 us -> 0.03 us
    unnamed x20 -> x12, local copies, waits for them, and re-layouts: 1.45 us -> 0.03 us
  transfers between devices with their start and end apart: 6 -> 6, of which waited for: 3 -> 3; matrix products, arithmetic and copies ran while one was open for 0% -> 0% of each run, Pallas kernels for 0% -> 1%
where the time goes in v4:
time: 119 us; the launch traced here: 118 us
  blocking collectives  58.5 us (49%)
  Pallas kernels  27.8 us (23%)
  starting transfers between devices  19.3 us (16%)
  waiting for transfers between devices  12.5 us (11%)
    all_to_all x1, blocking collectives, on_device(): lax.all_to_all(sending, 'col', split_axis=0, concat_axis=0, tiled=True, a...  58.5 us
    pallas_call x1, Pallas kernels, on_device(): pl.pallas_call(conv_kernel, out_shape=(jax.ShapeDtypeStruct((chips,) + ti...  22 us
    ppermute x4, starting transfers between devices, shifted(): return lax.ppermute(x, axis, pairs)  8.89 us
    all_to_all x1, starting transfers between devices, on_device(): lax.all_to_all(count, 'col', split_axis=0, concat_axis=0, tiled=True)  7.33 us
    all_to_all x1, waiting for transfers between devices, on_device(): lax.all_to_all(count, 'col', split_axis=0, concat_axis=0, tiled=True)  6.54 us
    ppermute x1, waiting for transfers between devices, on_device(): taken = lax.ppermute(give, 'col', [(i, i ^ 1) for i in range(columns)])  3.79 us
    ppermute x1, starting transfers between devices, on_device(): taken = lax.ppermute(give, 'col', [(i, i ^ 1) for i in range(columns)])  3.09 us
    pallas_call x1, Pallas kernels, on_device(): pl.pallas_call(rim_kernel, out_shape=(strip, strip, pair, pair, jax.Shape...  2.69 us
  transfers between devices with their start and end apart: 6, of which 3 were waited for; matrix products, arithmetic and copies ran while one was open for 0% of the time, Pallas kernels for 1%

profile of v4, /device:TPU:32, one launch (start us, length us, event | category | flops | bytes accessed | tf_op | source)
XLA Modules:
  0.0 118.5 jit_solution(6371717891615239619)
XLA Ops:
  0.0 0.0 copy-start.2
  0.0 0.0 copy-start.4
  0.0 0.0 copy-start.1
  0.0 0.0 copy-start.3
  0.0 0.0 copy-start
  0.0 2.7 %rim.1 = (bf16[528,128]{1,0:T(8,128)(2,1)S(1)}, bf16[528,128]{1,0:T(8,128)(2,1)S(1)}, bf16[2,64,128]{2,1,0:T(8,128)(2,1)S(1)}, bf16[2,64,128]{2,1,0:T(8,128)(2,1)S(1)}, f32[32,1,128]{2,1,0:T(1,128)}) custom-call(s32[2,8]{1,0:T(2,128)} %wet_ref.5, s32[2,2,8]{2,1,0:T(2,128)} %bitcast.5, bf16[2,8,32,32,128]{4,3,2,1,0:T(8,128)(2,1)} %fields_ref.3), custom_call_target="tpu_custom_call" | custom-call | tf_op jit(solution)/shard_map/rim/pallas_call | solution.py:467
  2.7 3.8 %collective-permute-start = (bf16[528,128]{1,0:T(8,128)(2,1)S(1)}, bf16[528,128]{1,0:T(8,128)(2,1)S(1)}, u32[]{:S(2)}, u32[]{:S(2)}) collective-permute-start(bf16[528,128]{1,0:T(8,128)(2,1)S(1)} %get-tuple-element.17), channel_id=1, source_target_pairs={{0,32},{32,64},{64,96},{1,33},{33,65},{65,97},{2,34},{34,66},{66,9... | collective-permute-start | bytes 405512 | tf_op jit(solution)/shard_map/ppermute | solution.py:447
  6.6 2.0 %collective-permute-start.1 = (bf16[528,128]{1,0:T(8,128)(2,1)S(1)}, bf16[528,128]{1,0:T(8,128)(2,1)S(1)}, u32[]{:S(2)}, u32[]{:S(2)}) collective-permute-start(bf16[528,128]{1,0:T(8,128)(2,1)S(1)} %get-tuple-element.18), channel_id=1, source_target_pairs={{32,0},{64,32},{96,64},{33,1},{65,33},{97,65},{34,2},{66,34},{98,6... | collective-permute-start | bytes 405512 | tf_op jit(solution)/shard_map/ppermute | solution.py:447
  8.6 7.3 %all-to-all-start = ((f32[32,1,128]{2,1,0:T(1,128)}), f32[32,1,128]{2,1,0:T(1,128)S(1)}, u32[]{:S(2)}, u32[]{:S(2)}) async-start(f32[32,1,128]{2,1,0:T(1,128)} %get-tuple-element.23), calls=%async_computation | async-start | bytes 32768 | tf_op jit(solution)/shard_map/all_to_all | solution.py:483
  15.9 0.0 collective-permute-done.north_ref
  15.9 0.0 collective-permute-done.1.south_ref
  15.9 0.7 side.1
  16.7 6.5 %all-to-all-done.count_ref = f32[32,1,128]{2,1,0:T(1,128)S(1)} async-done(((f32[32,1,128]{2,1,0:T(1,128)}), f32[32,1,128]{2,1,0:T(1,128)S(1)}, u32[]{:S(2)}, u32[]{:S(2)}) %all-to-all-start) | async-done | bytes 16416 | tf_op jit(solution)/shard_map/all_to_all | solution.py:483
  23.2 1.7 %collective-permute-start.2 = (bf16[160,128]{1,0:T(8,128)(2,1)S(1)}, bf16[160,128]{1,0:T(8,128)(2,1)S(1)}, u32[]{:S(2)}, u32[]{:S(2)}) collective-permute-start(bf16[160,128]{1,0:T(8,128)(2,1)S(1)} %get-tuple-element.25), channel_id=1, source_target_pairs={{0,1},{1,2},{2,3},{3,4},{4,5},{5,6},{6,7},{7,8},{8,9},{9,10},{10,1... | collective-permute-start | bytes 122888 | tf_op jit(solution)/shard_map/ppermute | solution.py:447
  25.0 1.3 %collective-permute-start.3 = (bf16[160,128]{1,0:T(8,128)(2,1)S(1)}, bf16[160,128]{1,0:T(8,128)(2,1)S(1)}, u32[]{:S(2)}, u32[]{:S(2)}) collective-permute-start(bf16[160,128]{1,0:T(8,128)(2,1)S(1)} %get-tuple-element.26), channel_id=1, source_target_pairs={{1,0},{2,1},{3,2},{4,3},{5,4},{6,5},{7,6},{8,7},{9,8},{10,9},{11,1... | collective-permute-start | bytes 122888 | tf_op jit(solution)/shard_map/ppermute | solution.py:447
  26.3 0.0 collective-permute-done.2.west_ref
  26.3 2.1 %collective-permute-done.3.east_ref = bf16[160,128]{1,0:T(8,128)(2,1)S(1)} collective-permute-done((bf16[160,128]{1,0:T(8,128)(2,1)S(1)}, bf16[160,128]{1,0:T(8,128)(2,1)S(1)}, u32[]{:S(2)}, u32[]{:S(2)}) %collective-permute-start.3) | collective-permute-done | bytes 40992 | tf_op jit(solution)/shard_map/ppermute | solution.py:447
  28.4 0.0 copy-done.2
  28.4 0.0 copy-done.4
  28.4 0.0 copy-done.1
  28.4 0.0 copy-done.3
  28.4 0.0 copy-done
  28.5 22.0 %both_convs.1 = (bf16[16,32,32,128]{3,2,1,0:T(8,128)(2,1)S(1)}, bf16[8,32,32,128]{3,2,1,0:T(8,128)(2,1)S(1)}) custom-call(s32[2,8]{1,0:T(2,128)} %wet_ref.5, s32[2,2,8]{2,1,0:T(2,128)} %bitcast.6, f32[32,1,128]{2,1,0:T(1,128)S(1)} %all-to-all-done.count_ref, bf16[2,8,32,32,128]{4,3,2,1,0:T(8,128)(2,1)} %fields_ref.3, ...), custom_call_target="tpu_custom_call" | custom-call | tf_op jit(solution)/shard_map/both_convs/pallas_call | solution.py:501
  50.5 3.1 %collective-permute-start.4 = (bf16[8,32,32,128]{3,2,1,0:T(8,128)(2,1)S(1)}, bf16[8,32,32,128]{3,2,1,0:T(8,128)(2,1)S(1)}, u32[]{:S(2)}, u32[]{:S(2)}) collective-permute-start(bf16[8,32,32,128]{3,2,1,0:T(8,128)(2,1)S(1)} %get-tuple-element.27), channel_id=1, source_target_pairs={{0,1},{1,0},{2,3},{3,2},{4,5},{5,4},{6,7},{7,6},{8,9},{9,8},{10,11... | collective-permute-start | bytes 6291464 | tf_op jit(solution)/shard_map/ppermute | solution.py:537
  53.5 3.8 %collective-permute-done.4.src_ref = bf16[8,32,32,128]{3,2,1,0:T(8,128)(2,1)S(1)} collective-permute-done((bf16[8,32,32,128]{3,2,1,0:T(8,128)(2,1)S(1)}, bf16[8,32,32,128]{3,2,1,0:T(8,128)(2,1)S(1)}, u32[]{:S(2)}, u32[]{:S(2)}) %collective-permute-start.4) | collective-permute-done | bytes 2097184 | tf_op jit(solution)/shard_map/ppermute | solution.py:537
  57.3 0.5 merge_mate.1
  57.8 0.0 copy-start.5
  57.9 58.5 %all_to_all.10.src_ref = bf16[16,32,32,128]{3,2,1,0:T(8,128)(2,1)S(1)} all-to-all(bf16[16,32,32,128]{3,2,1,0:T(8,128)(2,1)S(1)} %merge_mate.1), channel_id=1, replica_groups={{0,2,4,6,8,10,12,14,16,18,20,22,24,26,28,30},{1,3,5,7,9,11,13,15,17,19,..., dimensions={0} | all-to-all | bytes 8388608 | tf_op jit(solution)/shard_map/all_to_all | solution.py:549
  116.4 0.0 copy-done.5
  116.4 1.9 %slot_order.1 = bf16[8,32,32,128]{3,2,1,0:T(8,128)(2,1)} custom-call(s32[8]{0:T(128)S(1)} %copy-done.5, bf16[16,32,32,128]{3,2,1,0:T(8,128)(2,1)S(1)} %all_to_all.10.src_ref), custom_call_target="tpu_custom_call" | custom-call | tf_op jit(solution)/shard_map/slot_order/pallas_call | solution.py:552
Async XLA Ops:
  0.0 28.4 %copy-start.2 = (bf16[128,128]{1,0:T(8,128)(2,1)S(1)}, bf16[128,128]{1,0:T(8,128)(2,1)}, u32[]{:S(2)}) copy-start(bf16[128,128]{1,0:T(8,128)(2,1)} %mix_ref.1) | copy-start | bytes 98308
  0.0 28.4 %copy-start.4 = (f32[128]{0:T(128)S(1)}, f32[128]{0:T(128)}, u32[]{:S(2)}) copy-start(f32[128]{0:T(128)} %param.16) | copy-start | bytes 1540
  0.0 28.4 %copy-start.1 = (bf16[3,3,128,128]{3,2,1,0:T(8,128)(2,1)S(1)}, bf16[3,3,128,128]{3,2,1,0:T(8,128)(2,1)}, u32[]{:S(2)}) copy-start(bf16[3,3,128,128]{3,2,1,0:T(8,128)(2,1)} %k2_ref.1) | copy-start | bytes 884740
  0.0 28.4 %copy-start.3 = (f32[128]{0:T(128)S(1)}, f32[128]{0:T(128)}, u32[]{:S(2)}) copy-start(f32[128]{0:T(128)} %param.14) | copy-start | bytes 1540
  0.0 28.4 %copy-start = (bf16[3,3,128,128]{3,2,1,0:T(8,128)(2,1)S(1)}, bf16[3,3,128,128]{3,2,1,0:T(8,128)(2,1)}, u32[]{:S(2)}) copy-start(bf16[3,3,128,128]{3,2,1,0:T(8,128)(2,1)} %k1_ref.1) | copy-start | bytes 884740
  2.7 13.2 %collective-permute-start = (bf16[528,128]{1,0:T(8,128)(2,1)S(1)}, bf16[528,128]{1,0:T(8,128)(2,1)S(1)}, u32[]{:S(2)}, u32[]{:S(2)}) collective-permute-start(bf16[528,128]{1,0:T(8,128)(2,1)S(1)} %get-tuple-element.17), channel_id=1, source_target_pairs={{0,32},{32,64},{64,96},{1,33},{33,65},{65,97},{2,34},{34,66},{66,9... | collective-permute-start | bytes 405512 | tf_op jit(solution)/shard_map/ppermute | solution.py:447
  6.6 9.4 %collective-permute-start.1 = (bf16[528,128]{1,0:T(8,128)(2,1)S(1)}, bf16[528,128]{1,0:T(8,128)(2,1)S(1)}, u32[]{:S(2)}, u32[]{:S(2)}) collective-permute-start(bf16[528,128]{1,0:T(8,128)(2,1)S(1)} %get-tuple-element.18), channel_id=1, source_target_pairs={{32,0},{64,32},{96,64},{33,1},{65,33},{97,65},{34,2},{66,34},{98,6... | collective-permute-start | bytes 405512 | tf_op jit(solution)/shard_map/ppermute | solution.py:447
  8.6 14.6 %all-to-all-start = ((f32[32,1,128]{2,1,0:T(1,128)}), f32[32,1,128]{2,1,0:T(1,128)S(1)}, u32[]{:S(2)}, u32[]{:S(2)}) async-start(f32[32,1,128]{2,1,0:T(1,128)} %get-tuple-element.23), calls=%async_computation | async-start | bytes 32768 | tf_op jit(solution)/shard_map/all_to_all | solution.py:483
  23.2 3.1 %collective-permute-start.2 = (bf16[160,128]{1,0:T(8,128)(2,1)S(1)}, bf16[160,128]{1,0:T(8,128)(2,1)S(1)}, u32[]{:S(2)}, u32[]{:S(2)}) collective-permute-start(bf16[160,128]{1,0:T(8,128)(2,1)S(1)} %get-tuple-element.25), channel_id=1, source_target_pairs={{0,1},{1,2},{2,3},{3,4},{4,5},{5,6},{6,7},{7,8},{8,9},{9,10},{10,1... | collective-permute-start | bytes 122888 | tf_op jit(solution)/shard_map/ppermute | solution.py:447
  25.0 3.5 %collective-permute-start.3 = (bf16[160,128]{1,0:T(8,128)(2,1)S(1)}, bf16[160,128]{1,0:T(8,128)(2,1)S(1)}, u32[]{:S(2)}, u32[]{:S(2)}) collective-permute-start(bf16[160,128]{1,0:T(8,128)(2,1)S(1)} %get-tuple-element.26), channel_id=1, source_target_pairs={{1,0},{2,1},{3,2},{4,3},{5,4},{6,5},{7,6},{8,7},{9,8},{10,9},{11,1... | collective-permute-start | bytes 122888 | tf_op jit(solution)/shard_map/ppermute | solution.py:447
  50.5 6.9 %collective-permute-start.4 = (bf16[8,32,32,128]{3,2,1,0:T(8,128)(2,1)S(1)}, bf16[8,32,32,128]{3,2,1,0:T(8,128)(2,1)S(1)}, u32[]{:S(2)}, u32[]{:S(2)}) collective-permute-start(bf16[8,32,32,128]{3,2,1,0:T(8,128)(2,1)S(1)} %get-tuple-element.27), channel_id=1, source_target_pairs={{0,1},{1,0},{2,3},{3,2},{4,5},{5,4},{6,7},{7,6},{8,9},{9,8},{10,11... | collective-permute-start | bytes 6291464 | tf_op jit(solution)/shard_map/ppermute | solution.py:537
  57.8 58.6 %copy-start.5 = (s32[8]{0:T(128)S(1)}, s32[8]{0:T(128)}, u32[]{:S(2)}) copy-start(s32[8]{0:T(128)} %list_ref.1) | copy-start | bytes 100
